TPU v7x, 512 devices: a whole 4x8x8 slice. The times are simulated.
512 devices in a mesh: lat: 16 (over x, z_hi, core), lon: 32 (over y, z_lo).
Axes of the slice: x: 4, y: 8, z: 8 (z_hi: 2, z_lo: 4; z = z_hi * 4 + z_lo), core: 2. Of those that a mesh axis runs over, the one named last changes fastest.
Arguments:
- inputs_below: bfloat16 [64, 128, 4096], P(None, 'lat', 'lon'), may hold values from -6 to 6
- hidden_prev: bfloat16 [64, 128, 4096], P(None, 'lat', 'lon'), may hold values from -0.8984375 to 0.8984375
- cell_prev: float32 [64, 128, 4096], P(None, 'lat', 'lon'), may hold values from -5 to 5
- kernel_weights: bfloat16 [9, 256, 128], replicated, may hold values from -0.1875 to 0.1875
- gate_bias: float32 [256], replicated, may hold values from -4 to 4
- readout: float32 [64], replicated, may hold values from -0.75 to 0.75
- target_field: float32 [128, 4096], P('lat', 'lon'), may hold values from -6 to 6
- land_mask: int32 [128, 4096], P('lat', 'lon'), may hold values 0 or 1
- fire_mask: int32 [128, 4096], P('lat', 'lon'), may hold values 0 or 1
- hidden_grad: bfloat16 [64, 128, 4096], P(None, 'lat', 'lon'), may hold values from -10 to 10
Outputs:
- hidden_next: bfloat16 [64, 128, 4096], P(None, 'lat', 'lon')
- cell_next: float32 [64, 128, 4096], P(None, 'lat', 'lon')
- grad_inputs: bfloat16 [64, 128, 4096], P(None, 'lat', 'lon')
- grad_hidden: bfloat16 [64, 128, 4096], P(None, 'lat', 'lon')
- grad_cell: float32 [64, 128, 4096], P(None, 'lat', 'lon')
- grad_kernel: float32 [9, 256, 128], replicated
- grad_bias: float32 [256], replicated
Inputs may be any that keep to these rules, and one draw needn't show every extreme that they name: `land_mask`: 1 marks land cells, 0 sea cells. `fire_mask`: 1 marks cells where fire danger is observed.
All inputs are finite; a program needn't handle non-finite values. No bound on the sum of `land_mask` or of `fire_mask` on one device may be relied on, other than what follows from the above.
Results may differ from a plain program's by a relative error of at most 0.0049.
Values may be sent and summed in bfloat16 or wider, within the bound.
A program may use at most 64 MiB of HBM per device.

v0:
```python
import math

import jax
import jax.numpy as jnp
from jax import lax
from jax.sharding import PartitionSpec as P


def with_halo(cells, sides, width, closed):
    for axis, dim in sides:
        count = lax.axis_size(axis)
        ends = count if closed else count - 1
        head = lax.slice_in_dim(cells, 0, width, axis=dim)
        tail = lax.slice_in_dim(cells, cells.shape[dim] - width, cells.shape[dim], axis=dim)
        cells = jnp.concatenate(
            [
                lax.ppermute(tail, axis, [(i, (i + 1) % count) for i in range(ends)]),
                cells,
                lax.ppermute(head, axis, [((i + 1) % count, i) for i in range(ends)]),
            ],
            axis=dim,
        )
    return cells


def shifted(value, axis, steps):
    count = lax.axis_size(axis)
    pairs = [(source, (source + steps) % count) for source in range(count)]
    return lax.ppermute(value, axis, pairs)


def extend(field):
    banded = with_halo(field, (("lat", 1),), 1, False)
    edge_rows = jnp.concatenate([field[:, :1], field[:, -1:]], axis=1)
    across = shifted(edge_rows, "lon", lax.axis_size("lon") // 2)
    band_index = lax.axis_index("lat")
    northern = band_index == 0
    southern = band_index == lax.axis_size("lat") - 1
    top_row = jnp.where(northern, across[:, :1], banded[:, :1])
    bottom_row = jnp.where(southern, across[:, 1:], banded[:, -1:])
    joined = jnp.concatenate([top_row, banded[:, 1:-1], bottom_row], axis=1)
    return with_halo(joined, (("lon", 2),), 1, True)


def windows(padded, row_count, col_count, flipped):
    result = []
    for position in range(9):
        lat_start = position // 3
        lon_start = position % 3
        if flipped:
            lat_start = 2 - lat_start
            lon_start = 2 - lon_start
        result.append(
            padded[:, lat_start : lat_start + row_count, lon_start : lon_start + col_count]
        )
    return result


def body(
    inputs_below,
    hidden_prev,
    cell_prev,
    kernel_weights,
    gate_bias,
    readout,
    target_field,
    land_mask,
    fire_mask,
    hidden_grad,
):
    hidden_width = hidden_prev.shape[0]
    input_width = inputs_below.shape[0]
    gate_count = kernel_weights.shape[1]
    channels = kernel_weights.shape[2]
    row_count = cell_prev.shape[1]
    col_count = cell_prev.shape[2]
    stacked = jnp.concatenate([inputs_below, hidden_prev], axis=0)
    padded = extend(stacked)
    forward_windows = windows(padded, row_count, col_count, False)
    preact = jnp.zeros((gate_count, row_count, col_count), jnp.float32)
    for position in range(9):
        preact = preact + jnp.einsum(
            "gc,crw->grw",
            kernel_weights[position],
            forward_windows[position],
            preferred_element_type=jnp.float32,
        )
    preact = preact + gate_bias[:, None, None]
    input_gate = jax.nn.sigmoid(preact[0:hidden_width])
    forget_gate = jax.nn.sigmoid(preact[hidden_width : 2 * hidden_width])
    output_gate = jax.nn.sigmoid(preact[2 * hidden_width : 3 * hidden_width])
    candidate = jnp.tanh(preact[3 * hidden_width : 4 * hidden_width])
    land_float = land_mask.astype(jnp.float32)[None]
    fire_float = fire_mask.astype(jnp.float32)
    cell_next = land_float * (forget_gate * cell_prev + input_gate * candidate)
    squashed = jnp.tanh(cell_next)
    hidden_next = (output_gate * squashed).astype(jnp.bfloat16)
    predicted = jnp.sum(readout[:, None, None] * hidden_next.astype(jnp.float32), axis=0)
    total_grad = (
        hidden_grad.astype(jnp.float32)
        + 2.0 * (fire_float * (predicted - target_field))[None] * readout[:, None, None]
    )
    cell_grad = land_float * total_grad * output_gate * (1.0 - squashed * squashed)
    grad_cell = cell_grad * forget_gate
    pre_grad = jnp.concatenate(
        [
            cell_grad * candidate * input_gate * (1.0 - input_gate),
            cell_grad * cell_prev * forget_gate * (1.0 - forget_gate),
            total_grad * squashed * output_gate * (1.0 - output_gate),
            cell_grad * input_gate * (1.0 - candidate * candidate),
        ],
        axis=0,
    )
    pre_low = pre_grad.astype(jnp.bfloat16)
    local_bias = jnp.sum(pre_grad, axis=(1, 2))
    local_kernel = jnp.stack(
        [
            jnp.einsum(
                "grw,crw->gc",
                pre_low,
                forward_windows[position],
                preferred_element_type=jnp.float32,
            )
            for position in range(9)
        ],
        axis=0,
    )
    grad_padded = extend(pre_low)
    band_index = lax.axis_index("lat")
    northern = band_index == 0
    southern = band_index == lax.axis_size("lat") - 1
    row_index = lax.broadcasted_iota(jnp.int32, (1, row_count + 2, 1), 1)
    pole_rows = northern & (row_index == 0) | southern & (row_index == row_count + 1)
    main_padded = jnp.where(pole_rows, jnp.zeros_like(grad_padded), grad_padded)
    back_windows = windows(main_padded, row_count, col_count, True)
    field_grad = jnp.zeros((channels, row_count, col_count), jnp.float32)
    for position in range(9):
        field_grad = field_grad + jnp.einsum(
            "gc,grw->crw",
            kernel_weights[position],
            back_windows[position],
            preferred_element_type=jnp.float32,
        )
    north_term = jnp.zeros((channels, col_count), jnp.float32)
    south_term = jnp.zeros((channels, col_count), jnp.float32)
    for position in range(3):
        lon_start = 2 - position
        north_term = north_term + jnp.einsum(
            "gc,gw->cw",
            kernel_weights[position],
            grad_padded[:, 0, lon_start : lon_start + col_count],
            preferred_element_type=jnp.float32,
        )
        south_term = south_term + jnp.einsum(
            "gc,gw->cw",
            kernel_weights[6 + position],
            grad_padded[:, row_count + 1, lon_start : lon_start + col_count],
            preferred_element_type=jnp.float32,
        )
    field_grad = field_grad.at[:, 0].add(jnp.where(northern, north_term, 0.0))
    field_grad = field_grad.at[:, row_count - 1].add(jnp.where(southern, south_term, 0.0))
    grad_inputs = field_grad[:input_width].astype(jnp.bfloat16)
    grad_hidden = field_grad[input_width:].astype(jnp.bfloat16)
    scaling = 1.0 / math.sqrt(row_count * lax.axis_size("lat") * col_count * lax.axis_size("lon"))
    summed_kernel, summed_bias = lax.psum((local_kernel, local_bias), ("lat", "lon"))
    grad_kernel = summed_kernel * scaling
    grad_bias = summed_bias * scaling
    return (hidden_next, cell_next, grad_inputs, grad_hidden, grad_cell, grad_kernel, grad_bias)


def solution(mesh):
    return jax.shard_map(
        body,
        mesh=mesh,
        in_specs=(
            P(None, "lat", "lon"),
            P(None, "lat", "lon"),
            P(None, "lat", "lon"),
            P(),
            P(),
            P(),
            P("lat", "lon"),
            P("lat", "lon"),
            P("lat", "lon"),
            P(None, "lat", "lon"),
        ),
        out_specs=(
            P(None, "lat", "lon"),
            P(None, "lat", "lon"),
            P(None, "lat", "lon"),
            P(None, "lat", "lon"),
            P(None, "lat", "lon"),
            P(),
            P(),
        ),
        check_vma=False,
    )
```

profile of v0, /device:TPU:1, one launch (start us, length us, event | category | flops | bytes accessed | tf_op | source)
XLA Modules:
  0.0 486.5 jit_solution(17038042296153973256)
XLA Ops:
  7.2 1.1 copy.215
  8.4 1.1 copy.216
  9.6 12.0 %collective-permute-start.1 = (bf16[128,1,128]{0,2,1:T(8,128)(2,1)S(1)}, bf16[128,1,128]{0,2,1:T(8,128)(2,1)S(1)}, u32[]{:S(2)}, u32[]{:S(2)}) collective-permute-start(bf16[128,1,128]{0,2,1:T(8,128)(2,1)S(1)} %get-tuple-element.98), channel_id=1, source_target_pairs={{0,32},{32,64},{64,96},{96,128},{128,160},{160,192},{192,224},{224... | collective-permute-start | bytes 98312 | tf_op jit(solution)/shard_map/ppermute | solution.py:17
  21.6 1.9 collective-permute-start.2
  23.6 7.5 %collective-permute-start = (bf16[128,2,128]{0,2,1:T(8,128)(2,1)S(1)}, bf16[128,2,128]{0,2,1:T(8,128)(2,1)S(1)}, u32[]{:S(2)}, u32[]{:S(2)}) collective-permute-start(bf16[128,2,128]{0,2,1:T(8,128)(2,1)S(1)} %pad_maximum_fusion.13), channel_id=1, source_target_pairs={{0,16},{1,17},{2,18},{3,19},{4,20},{5,21},{6,22},{7,23},{8,24},{9,... | collective-permute-start | bytes 196616 | tf_op jit(solution)/shard_map/ppermute | solution.py:29
  31.0 0.3 fusion.105
  31.4 1.3 copy.221
  32.8 0.3 fusion.30
  33.2 3.1 collective-permute-start.3
  36.3 7.1 %collective-permute-start.4 = (bf16[128,10,1]{0,2,1:T(2,128)(2,1)S(1)}, bf16[128,10,1]{0,2,1:T(2,128)(2,1)S(1)}, u32[]{:S(2)}, u32[]{:S(2)}) collective-permute-start(bf16[128,10,1]{0,2,1:T(2,128)(2,1)S(1)} %get-tuple-element.95), channel_id=1, source_target_pairs={{1,0},{2,1},{3,2},{4,3},{5,4},{6,5},{7,6},{8,7},{9,8},{10,9},{11,1... | collective-permute-start | bytes 7688 | tf_op jit(solution)/shard_map/ppermute | solution.py:19
  43.4 0.4 fusion.36
  43.8 1.3 copy.218
  45.1 1.3 copy.224
  46.4 0.3 maximum_maximum_fusion
  46.8 1.3 fusion.77
  48.1 0.3 fusion.71
  48.4 1.3 fusion.74
  49.6 1.4 fusion.68
  51.0 1.3 fusion.65
  52.3 0.3 fusion.62
  52.6 2.5 copy.217
  55.1 2.6 copy.219
  57.7 1.3 copy.220
  59.0 2.6 copy.222
  61.6 1.4 copy.223
  63.1 1.3 copy.225
  64.4 3.9 add_bitcast_fusion
  68.3 1.0 multiply_reduce_fusion
  69.3 0.9 fusion.157
  70.6 0.9 copy-done.7
  71.5 0.9 fusion.9
  72.6 9.0 %collective-permute-start.6 = (bf16[256,1,128]{2,1,0:T(2,128)(2,1)S(1)}, bf16[256,1,128]{2,1,0:T(2,128)(2,1)S(1)}, u32[]{:S(2)}, u32[]{:S(2)}) collective-permute-start(bf16[256,1,128]{2,1,0:T(2,128)(2,1)S(1)} %get-tuple-element.96), channel_id=1, source_target_pairs={{0,32},{32,64},{64,96},{96,128},{128,160},{160,192},{192,224},{224... | collective-permute-start | bytes 196616 | tf_op jit(solution)/shard_map/ppermute | solution.py:17
  81.6 0.3 pad_maximum_fusion.12
  81.9 1.9 collective-permute-start.7
  83.8 1.0 fusion.8
  84.8 1.0 fusion.7
  85.8 0.9 fusion.6
  86.7 1.0 fusion.5
  87.8 1.0 fusion.4
  88.8 0.9 fusion.3
  89.7 1.0 fusion.2
  90.8 7.1 %collective-permute-start.5 = (bf16[256,2,128]{2,1,0:T(2,128)(2,1)S(1)}, bf16[256,2,128]{2,1,0:T(2,128)(2,1)S(1)}, u32[]{:S(2)}, u32[]{:S(2)}) collective-permute-start(bf16[256,2,128]{2,1,0:T(2,128)(2,1)S(1)} %pad_maximum_fusion.12), channel_id=1, source_target_pairs={{0,16},{1,17},{2,18},{3,19},{4,20},{5,21},{6,22},{7,23},{8,24},{9,... | collective-permute-start | bytes 393224 | tf_op jit(solution)/shard_map/ppermute | solution.py:29
  97.9 1.0 fusion.1
  98.9 1.0 fusion.18
  99.9 98.2 %psum.15 = f32[256]{0:T(256)S(1)} all-reduce(f32[256]{0:T(256)S(1)} %fusion.18), channel_id=1, replica_groups=mesh['lat'=16,'lon'=32] {'lat','lon'}, use_global_device_ids=true, to_apply=%region_3.4 | all-reduce | flops 256 | bytes 2048 | tf_op jit(solution)/shard_map/psum | solution.py:165
  198.1 0.4 broadcast_select_fusion.1
  198.5 0.6 pad_maximum_fusion.1
  199.2 0.5 fusion.159
  199.6 0.9 copy.226
  200.5 3.2 collective-permute-start.8
  203.8 0.9 copy.227
  204.7 5.9 %collective-permute-start.9 = (bf16[256,10,1]{0,1,2:T(8,128)(2,1)S(1)}, bf16[256,10,1]{0,1,2:T(8,128)(2,1)S(1)}, u32[]{:S(2)}, u32[]{:S(2)}) collective-permute-start(bf16[256,10,1]{0,1,2:T(8,128)(2,1)S(1)} %copy.227), channel_id=1, source_target_pairs={{1,0},{2,1},{3,2},{4,3},{5,4},{6,5},{7,6},{8,7},{9,8},{10,9},{11,1... | collective-permute-start | bytes 15368 | tf_op jit(solution)/shard_map/ppermute | solution.py:19
  210.6 0.6 broadcast_multiply_fusion.1
  211.2 1.0 copy.228
  212.3 1.0 copy.229
  213.3 1.5 pad_maximum_fusion.4
  215.5 2.7 maximum_select_fusion
  218.2 1.4 fusion.158
  221.0 0.3 convolution_add_fusion.3
  221.3 0.3 convolution_add_fusion.2
  222.9 0.7 copy.268
  223.6 0.7 copy.269
  224.4 252.9 %all-reduce.2.cloned.1.call-done = f32[9,256,128]{2,1,0:T(8,128)} async-done(((f32[9,256,128]{2,1,0:T(8,128)}), f32[9,256,128]{2,1,0:T(8,128)}) %all-reduce.2.cloned.1.call-update) | async-done | bytes 1179664 | tf_op jit(solution)/shard_map/psum | solution.py:165
  477.3 2.4 broadcast_multiply_fusion
  (68 shorter events, 4.1 us)
Async XLA Ops:
  7.2 23.9 %copy-start.1 = (bf16[9,256,128]{2,1,0:T(8,128)(2,1)S(1)}, bf16[9,256,128]{2,1,0:T(8,128)(2,1)}, u32[]{:S(2)}) copy-start(bf16[9,256,128]{2,1,0:T(8,128)(2,1)} %param.17) | copy-start | bytes 1769476
  7.2 470.1 %all-reduce.2.cloned.1.call-start = ((), (), s32[]{:S(2)}) async-start(), calls=%async_computation | async-start | bytes 2359296 | tf_op jit(solution)/shard_map/psum | solution.py:165
  9.6 23.2 %collective-permute-start.1 = (bf16[128,1,128]{0,2,1:T(8,128)(2,1)S(1)}, bf16[128,1,128]{0,2,1:T(8,128)(2,1)S(1)}, u32[]{:S(2)}, u32[]{:S(2)}) collective-permute-start(bf16[128,1,128]{0,2,1:T(8,128)(2,1)S(1)} %get-tuple-element.98), channel_id=1, source_target_pairs={{0,32},{32,64},{64,96},{96,128},{128,160},{160,192},{192,224},{224... | collective-permute-start | bytes 98312 | tf_op jit(solution)/shard_map/ppermute | solution.py:17
  21.6 11.1 %collective-permute-start.2 = (bf16[128,1,128]{0,2,1:T(8,128)(2,1)S(1)}, bf16[128,1,128]{0,2,1:T(8,128)(2,1)S(1)}, u32[]{:S(2)}, u32[]{:S(2)}) collective-permute-start(bf16[128,1,128]{0,2,1:T(8,128)(2,1)S(1)} %get-tuple-element.99), channel_id=1, source_target_pairs={{32,0},{64,32},{96,64},{128,96},{160,128},{192,160},{224,192},{256... | collective-permute-start | bytes 98312 | tf_op jit(solution)/shard_map/ppermute | solution.py:19
  23.6 9.2 %collective-permute-start = (bf16[128,2,128]{0,2,1:T(8,128)(2,1)S(1)}, bf16[128,2,128]{0,2,1:T(8,128)(2,1)S(1)}, u32[]{:S(2)}, u32[]{:S(2)}) collective-permute-start(bf16[128,2,128]{0,2,1:T(8,128)(2,1)S(1)} %pad_maximum_fusion.13), channel_id=1, source_target_pairs={{0,16},{1,17},{2,18},{3,19},{4,20},{5,21},{6,22},{7,23},{8,24},{9,... | collective-permute-start | bytes 196616 | tf_op jit(solution)/shard_map/ppermute | solution.py:29
  31.4 1.3 copy-start.11
  33.2 13.2 %collective-permute-start.3 = (bf16[128,10,1]{0,2,1:T(2,128)(2,1)S(1)}, bf16[128,10,1]{0,2,1:T(2,128)(2,1)S(1)}, u32[]{:S(2)}, u32[]{:S(2)}) collective-permute-start(bf16[128,10,1]{0,2,1:T(2,128)(2,1)S(1)} %get-tuple-element.94), channel_id=1, source_target_pairs={{0,1},{1,2},{2,3},{3,4},{4,5},{5,6},{6,7},{7,8},{8,9},{9,10},{10,1... | collective-permute-start | bytes 7688 | tf_op jit(solution)/shard_map/ppermute | solution.py:17
  36.3 10.1 %collective-permute-start.4 = (bf16[128,10,1]{0,2,1:T(2,128)(2,1)S(1)}, bf16[128,10,1]{0,2,1:T(2,128)(2,1)S(1)}, u32[]{:S(2)}, u32[]{:S(2)}) collective-permute-start(bf16[128,10,1]{0,2,1:T(2,128)(2,1)S(1)} %get-tuple-element.95), channel_id=1, source_target_pairs={{1,0},{2,1},{3,2},{4,3},{5,4},{6,5},{7,6},{8,7},{9,8},{10,9},{11,1... | collective-permute-start | bytes 7688 | tf_op jit(solution)/shard_map/ppermute | solution.py:19
  46.8 4.3 copy-start.6
  46.8 5.5 %copy-start.4 = (bf16[128,10,129]{0,2,1:T(8,128)(2,1)}, bf16[128,10,129]{0,2,1:T(8,128)(2,1)S(1)}, u32[]{:S(2)}) copy-start(bf16[128,10,129]{0,2,1:T(8,128)(2,1)S(1)} %get-tuple-element.93) | copy-start | bytes 990724
  59.0 2.6 copy-start
  63.1 1.3 copy-start.3
  63.1 1.3 copy-start.15
  64.4 3.9 copy-start.9
  64.4 3.9 copy-start.14
  68.3 1.0 copy-start.12
  68.3 1.0 copy-start.13
  68.3 1.0 copy-start.10
  69.3 1.2 copy-start.8
  70.5 1.0 copy-start.7
  72.4 12.4 %copy-start.5 = (bf16[128,10,129]{0,2,1:T(8,128)(2,1)S(1)}, bf16[128,10,129]{0,2,1:T(8,128)(2,1)}, u32[]{:S(2)}) copy-start(bf16[128,10,129]{0,2,1:T(8,128)(2,1)} %copy-done.4) | copy-start | bytes 990724
  72.6 125.5 %collective-permute-start.6 = (bf16[256,1,128]{2,1,0:T(2,128)(2,1)S(1)}, bf16[256,1,128]{2,1,0:T(2,128)(2,1)S(1)}, u32[]{:S(2)}, u32[]{:S(2)}) collective-permute-start(bf16[256,1,128]{2,1,0:T(2,128)(2,1)S(1)} %get-tuple-element.96), channel_id=1, source_target_pairs={{0,32},{32,64},{64,96},{96,128},{128,160},{160,192},{192,224},{224... | collective-permute-start | bytes 196616 | tf_op jit(solution)/shard_map/ppermute | solution.py:17
  81.9 116.2 %collective-permute-start.7 = (bf16[256,1,128]{2,1,0:T(2,128)(2,1)S(1)}, bf16[256,1,128]{2,1,0:T(2,128)(2,1)S(1)}, u32[]{:S(2)}, u32[]{:S(2)}) collective-permute-start(bf16[256,1,128]{2,1,0:T(2,128)(2,1)S(1)} %get-tuple-element.97), channel_id=1, source_target_pairs={{32,0},{64,32},{96,64},{128,96},{160,128},{192,160},{224,192},{256... | collective-permute-start | bytes 196616 | tf_op jit(solution)/shard_map/ppermute | solution.py:19
  90.8 107.3 %collective-permute-start.5 = (bf16[256,2,128]{2,1,0:T(2,128)(2,1)S(1)}, bf16[256,2,128]{2,1,0:T(2,128)(2,1)S(1)}, u32[]{:S(2)}, u32[]{:S(2)}) collective-permute-start(bf16[256,2,128]{2,1,0:T(2,128)(2,1)S(1)} %pad_maximum_fusion.12), channel_id=1, source_target_pairs={{0,16},{1,17},{2,18},{3,19},{4,20},{5,21},{6,22},{7,23},{8,24},{9,... | collective-permute-start | bytes 393224 | tf_op jit(solution)/shard_map/ppermute | solution.py:29
  200.5 10.7 %collective-permute-start.8 = (bf16[256,10,1]{0,1,2:T(8,128)(2,1)S(1)}, bf16[256,10,1]{0,1,2:T(8,128)(2,1)S(1)}, u32[]{:S(2)}, u32[]{:S(2)}) collective-permute-start(bf16[256,10,1]{0,1,2:T(8,128)(2,1)S(1)} %copy.226), channel_id=1, source_target_pairs={{0,1},{1,2},{2,3},{3,4},{4,5},{5,6},{6,7},{7,8},{8,9},{9,10},{10,1... | collective-permute-start | bytes 15368 | tf_op jit(solution)/shard_map/ppermute | solution.py:17
  204.7 7.6 %collective-permute-start.9 = (bf16[256,10,1]{0,1,2:T(8,128)(2,1)S(1)}, bf16[256,10,1]{0,1,2:T(8,128)(2,1)S(1)}, u32[]{:S(2)}, u32[]{:S(2)}) collective-permute-start(bf16[256,10,1]{0,1,2:T(8,128)(2,1)S(1)} %copy.227), channel_id=1, source_target_pairs={{1,0},{2,1},{3,2},{4,3},{5,4},{6,5},{7,6},{8,7},{9,8},{10,9},{11,1... | collective-permute-start | bytes 15368 | tf_op jit(solution)/shard_map/ppermute | solution.py:19
  213.3 1.6 copy-start.2
Sparse Core Ops, SparseCore 0:
  211.3 265.8 all-reduce.1
where the time goes:
time: 487 us; the launch traced here: 486 us
  waiting for transfers between devices  253 us (52%)
  blocking collectives  98.2 us (20%)
  starting transfers between devices  58.8 us (12%)
  local copies, waits for them, and re-layouts  26.3 us (5%)
  matrix products  19.5 us (4%)
  other arithmetic  16.2 us (3%)
  between operations  14.6 us (3%)
    psum x1, waiting for transfers between devices, body(): lax.psum((local_kernel, local_bias), ('lat', 'lon'))  253 us
    psum x1, blocking collectives, body(): lax.psum((local_kernel, local_bias), ('lat', 'lon'))  98.2 us
    ppermute x4, starting transfers between devices, with_halo(): lax.ppermute(tail, axis, [(i, (i + 1) % count) for i in range(ends)])  27.3 us
    ppermute x4, starting transfers between devices, with_halo(): lax.ppermute(head, axis, [((i + 1) % count, i) for i in range(ends)])  16.8 us
    dot_general x9, local copies, waits for them, and re-layouts, body(): jnp.einsum('gc,crw->grw', kernel_weights[position], forward_windows[posit...  15.7 us
    ppermute x2, starting transfers between devices, shifted(): return lax.ppermute(value, axis, pairs)  14.6 us
  transfers between devices with their start and end apart: 11, of which 1 were waited for; matrix products, arithmetic and copies ran while one was open for 6% of the time, Pallas kernels for 0%

commit v1 on v0

v1 whole, which is shorter than its diff:
```python
import functools
import math

import jax
import jax.numpy as jnp
from jax import lax
from jax.experimental import pallas as pl
from jax.experimental.pallas import tpu as pltpu
from jax.sharding import PartitionSpec as P

MESH = pl.DeviceIdType.MESH
F32 = jnp.float32
BF16 = jnp.bfloat16
ROWS = 8
COLS = 128
PADDED = ROWS + 2
STATE = 128
GATES = 256
HALF = GATES // 2
LANES = 128
VMEM_SPEC = pl.BlockSpec(memory_space=pltpu.VMEM)
VMEM_LIMIT = 48 * 1024 * 1024


class Place:
    def __init__(self, sizes):
        self.nx, self.ny, self.zh, self.zl = sizes
        self.nz = self.zh * self.zl
        self.nlat = self.nx * self.zh * 2
        self.nlon = self.ny * self.zl
        self.lat = lax.axis_index("lat")
        self.lon = lax.axis_index("lon")
        self.core = lax.rem(self.lat, 2)
        chip = self.lat // 2
        self.z_hi = lax.rem(chip, self.zh)
        self.x = chip // self.zh
        self.z_lo = lax.rem(self.lon, self.zl)
        self.y = self.lon // self.zl
        self.z = self.z_hi * self.zl + self.z_lo
        self.count = {"core": 2, "x": self.nx, "y": self.ny, "z": self.nz}
        self.index = {"core": self.core, "x": self.x, "y": self.y, "z": self.z}
        self.north = self.lat == 0
        self.south = self.lat == self.nlat - 1

    def at(self, x, y, z, core):
        lat = (x * self.zh + z // self.zl) * 2 + core
        lon = y * self.zl + lax.rem(z, self.zl)
        return (lat, lon)

    def peer(self, axis, steps):
        other = lax.rem(self.index[axis] + steps, self.count[axis])
        where = dict(self.index)
        where[axis] = other
        return self.at(where["x"], where["y"], where["z"], where["core"]), other

    def peers(self, axis):
        return [self.peer(axis, steps) for steps in range(1, self.count[axis])]

    def up(self):
        opposite = lax.rem(self.lon + self.nlon // 2, self.nlon)
        lat = jnp.where(self.north, 0, self.lat - 1)
        return (lat, jnp.where(self.north, opposite, self.lon))

    def down(self):
        opposite = lax.rem(self.lon + self.nlon // 2, self.nlon)
        lat = jnp.where(self.south, self.nlat - 1, self.lat + 1)
        return (lat, jnp.where(self.south, opposite, self.lon))

    def east(self):
        return (self.lat, lax.rem(self.lon + 1, self.nlon))

    def west(self):
        return (self.lat, lax.rem(self.lon + self.nlon - 1, self.nlon))

    def around(self):
        return [self.up(), self.down(), self.east(), self.west()]


def greet(devices):
    barrier = pltpu.get_barrier_semaphore()
    for device in devices:
        pl.semaphore_signal(barrier, inc=1, device_id=device, device_id_type=MESH)
    return barrier


def remote(source, target, send_sem, recv_sem, device):
    return pltpu.make_async_remote_copy(
        src_ref=source,
        dst_ref=target,
        send_sem=send_sem,
        recv_sem=recv_sem,
        device_id=device,
        device_id_type=MESH,
    )


def lane_ids(shape):
    return lax.broadcasted_iota(jnp.int32, shape, len(shape) - 1)


def rows_out(place, first, last, halo, send_sem, recv_sem):
    upper_slot = jnp.where(place.north, 0, 1)
    lower_slot = jnp.where(place.south, 1, 0)
    copies = [
        remote(first, halo.at[upper_slot], send_sem.at[0], recv_sem.at[upper_slot], place.up()),
        remote(last, halo.at[lower_slot], send_sem.at[1], recv_sem.at[lower_slot], place.down()),
    ]
    for copy in copies:
        copy.start()
    waits = [
        remote(first, halo.at[0], send_sem.at[0], recv_sem.at[0], place.up()),
        remote(last, halo.at[1], send_sem.at[1], recv_sem.at[1], place.down()),
    ]
    return copies, waits


def collect(total, row, position, shift, lanes):
    return jnp.where(lanes == position, pltpu.roll(row, shift % LANES, 1), total)


def cols_out(place, edges, sides, send_sem, recv_sem):
    copies = [
        remote(edges.at[0], sides.at[0], send_sem.at[0], recv_sem.at[0], place.east()),
        remote(edges.at[1], sides.at[1], send_sem.at[1], recv_sem.at[1], place.west()),
    ]
    for copy in copies:
        copy.start()
    return copies


def halo_kernel(sizes, below, hidden, rows, sides, wide, halo, edges, row_send, row_recv, col_send, col_recv):
    place = Place(sizes)
    barrier = greet(place.around())
    width = below.shape[0]
    wide[pl.ds(0, width * ROWS), :] = below[...].astype(F32).reshape(width * ROWS, COLS)
    wide[pl.ds(width * ROWS, width * ROWS), :] = hidden[...].astype(F32).reshape(width * ROWS, COLS)

    def row_of(r):
        return wide[pl.ds(r, STATE, stride=ROWS), :]

    for r in (0, ROWS - 1):
        rows[r + 1] = row_of(r).astype(BF16)
    pl.semaphore_wait(barrier, 4)
    copies, waits = rows_out(place, rows.at[1], rows.at[ROWS], halo, row_send, row_recv)
    lanes = lane_ids((STATE, COLS))
    east = jnp.zeros((STATE, COLS), F32)
    west = jnp.zeros((STATE, COLS), F32)
    for r in range(ROWS):
        value = row_of(r)
        if 0 < r < ROWS - 1:
            rows[r + 1] = value.astype(BF16)
        east = collect(east, value, r + 1, r + 2, lanes)
        west = collect(west, value, r + 1, r + 1, lanes)
    for slot, position in ((0, 0), (1, ROWS + 1)):
        waits[slot].wait_recv()
        value = halo[slot].astype(F32)
        rows[position] = halo[slot]
        east = collect(east, value, position, position + 1, lanes)
        west = collect(west, value, position, position, lanes)
    edges[0] = east.astype(BF16)
    edges[1] = west.astype(BF16)
    col_copies = cols_out(place, edges, sides, col_send, col_recv)
    for copy in copies:
        copy.wait_send()
    for copy in col_copies:
        copy.wait()


def spread(values, sides_low, sides_high, lanes, position):
    before = jnp.where(lanes == 0, pltpu.roll(sides_low, (-position) % LANES, 1), pltpu.roll(values, 1, 1))
    after = jnp.where(
        lanes == COLS - 1, pltpu.roll(sides_high, (COLS - 1 - position) % LANES, 1), pltpu.roll(values, COLS - 1, 1)
    )
    return before, after


def local_kernel(
    rows,
    sides,
    cell_prev,
    hidden_grad,
    weights,
    gate_bias,
    readout,
    target,
    land,
    fire,
    hidden_next,
    cell_next,
    grad_cell,
    kernel_part,
    bias_part,
    low_rows,
    low_edges,
    windows,
    wide_grad,
    wide_next,
):
    hid = hidden_next.shape[0]
    lanes = lane_ids((STATE, COLS))
    low_side = sides[0].astype(F32)
    high_side = sides[1].astype(F32)
    for position in range(PADDED):
        value = rows[position].astype(F32)
        before, after = spread(value, low_side, high_side, lanes, position)
        windows[position, 0:STATE] = before.astype(BF16)
        windows[position, STATE : 2 * STATE] = rows[position]
        windows[position, 2 * STATE : 3 * STATE] = after.astype(BF16)
    wide_grad[...] = hidden_grad[...].astype(F32).reshape(hid * ROWS, COLS)
    flat = jnp.concatenate([weights[t] for t in range(9)], axis=1)
    bias_cols = jnp.transpose(jnp.broadcast_to(gate_bias[...], (LANES, GATES)))
    read_cols = jnp.transpose(jnp.broadcast_to(readout[...], (LANES, LANES)))[0:hid]
    bias_sum = jnp.zeros((GATES, COLS), F32)
    gate_lanes = lane_ids((GATES, COLS))
    east = jnp.zeros((GATES, COLS), F32)
    west = jnp.zeros((GATES, COLS), F32)
    for pair in range(ROWS // 2):
        first = 2 * pair
        columns = jnp.concatenate(
            [windows[first + k : first + k + 3].reshape(9 * STATE, COLS) for k in range(2)], axis=1
        )
        both = jnp.dot(flat, columns, preferred_element_type=F32)
        for k in range(2):
            r = first + k
            preact = both[:, k * COLS : (k + 1) * COLS] + bias_cols
            input_gate = jax.nn.sigmoid(preact[0:hid])
            forget_gate = jax.nn.sigmoid(preact[hid : 2 * hid])
            output_gate = jax.nn.sigmoid(preact[2 * hid : 3 * hid])
            candidate = jnp.tanh(preact[3 * hid : 4 * hid])
            land_row = land[r : r + 1, :].astype(F32)
            fire_row = fire[r : r + 1, :].astype(F32)
            prev = cell_prev[pl.ds(r, hid, stride=ROWS), :]
            cell = land_row * (forget_gate * prev + input_gate * candidate)
            squashed = jnp.tanh(cell)
            hidden = (output_gate * squashed).astype(BF16).astype(F32)
            predicted = jnp.sum(read_cols * hidden, axis=0, keepdims=True)
            miss = 2.0 * (fire_row * (predicted - target[r : r + 1, :]))
            total_grad = wide_grad[pl.ds(r, hid, stride=ROWS), :] + miss * read_cols
            cell_grad = land_row * total_grad * output_gate * (1.0 - squashed * squashed)
            pre_grad = jnp.concatenate(
                [
                    cell_grad * candidate * input_gate * (1.0 - input_gate),
                    cell_grad * prev * forget_gate * (1.0 - forget_gate),
                    total_grad * squashed * output_gate * (1.0 - output_gate),
                    cell_grad * input_gate * (1.0 - candidate * candidate),
                ],
                axis=0,
            )
            cell_next[pl.ds(r, hid, stride=ROWS), :] = cell
            grad_cell[pl.ds(r, hid, stride=ROWS), :] = cell_grad * forget_gate
            wide_next[pl.ds(r, hid, stride=ROWS), :] = hidden
            bias_sum = bias_sum + pre_grad
            low = pre_grad.astype(BF16)
            low_rows[r] = low
            rounded = low.astype(F32)
            east = collect(east, rounded, r + 1, r + 2, gate_lanes)
            west = collect(west, rounded, r + 1, r + 1, gate_lanes)
    hidden_next[...] = wide_next[...].reshape(hid, ROWS, COLS).astype(BF16)
    low_edges[0] = east
    low_edges[1] = west
    bias_part[...] = lax.dot_general(
        jnp.ones((8, COLS), F32),
        bias_sum,
        (((1,), (1,)), ((), ())),
        precision=lax.Precision.HIGHEST,
        preferred_element_type=F32,
    )
    cells = jnp.concatenate([low_rows[r] for r in range(ROWS)], axis=1)
    for a in range(3):
        seen = jnp.concatenate([windows[r + a] for r in range(ROWS)], axis=1)
        part = lax.dot_general(cells, seen, (((1,), (1,)), ((), ())), preferred_element_type=F32)
        for b in range(3):
            kernel_part[3 * a + b] = part[:, b * STATE : (b + 1) * STATE]


ORDERS = (("y", "z", "x"), ("z", "x", "y"), ("x", "y", "z"))


def reduce_kernel(
    sizes,
    scaling,
    kernel_part,
    bias_part,
    low_rows,
    low_edges,
    kernel_sum,
    bias_sum,
    halo,
    sides,
    pair_in,
    owned,
    bias_at,
    edges,
    first_in,
    second_out,
    second_in,
    third,
    gathered,
    bias_bufs,
    row_send,
    row_recv,
    col_send,
    col_recv,
    sends,
    recvs,
    bias_send,
    bias_recv,
):
    place = Place(sizes)
    partner, _ = place.peer("core", 1)
    devices = [partner] + place.around()
    for axis in ("x", "y", "z"):
        devices += [device for device, _ in place.peers(axis)]
    barrier = greet(devices)
    mine = pl.multiple_of(place.core * HALF, HALF)
    theirs = pl.multiple_of((1 - place.core) * HALF, HALF)
    pending = []
    pl.semaphore_wait(barrier, len(devices))

    pair_copies = []
    for a in range(3):
        copy = remote(
            kernel_part.at[pl.ds(3 * a, 3), pl.ds(theirs, HALF), :],
            pair_in.at[a],
            sends.at[0, a, 0],
            recvs.at[0, a, 0],
            partner,
        )
        copy.start()
        pair_copies.append(copy)

    def bias_start(stage, axis, value):
        slot = place.index[axis]
        buf = bias_bufs[stage]
        buf[slot] = value
        copies = []
        for k, (device, _) in enumerate(place.peers(axis)):
            copy = remote(buf.at[slot], buf.at[slot], bias_send.at[stage, k], bias_recv.at[stage, k], device)
            copy.start()
            copies.append(copy)
        return copies

    def bias_finish(stage, axis, copies):
        buf = bias_bufs[stage]
        for copy in copies:
            copy.wait_recv()
        pending.extend(copies)
        total = buf[0]
        for k in range(1, place.count[axis]):
            total = total + buf[k]
        return total

    bias_copies = bias_start(0, "core", bias_part[...])
    row_copies, row_waits = rows_out(place, low_rows.at[0], low_rows.at[ROWS - 1], halo, row_send, row_recv)

    first_copies = []
    for a in range(3):
        pair_copies[a].wait_recv()
        for b in range(3):
            owned[a, b] = kernel_part[3 * a + b, pl.ds(mine, HALF), :] + pair_in[a, b]
        axis = ORDERS[a][0]
        rows1 = HALF // place.count[axis]
        copies = []
        for k, (device, other) in enumerate(place.peers(axis)):
            start = pl.multiple_of(other * rows1, rows1)
            copy = remote(
                owned.at[a, :, pl.ds(start, rows1), :],
                first_in[a].at[k],
                sends.at[1, a, k],
                recvs.at[1, a, k],
                device,
            )
            copy.start()
            copies.append(copy)
        first_copies.append(copies)
    pending.extend(pair_copies)

    bias = bias_finish(0, "core", bias_copies)
    bias_copies = bias_start(1, "x", bias)

    lanes = lane_ids((GATES, COLS))
    east, west = low_edges[0], low_edges[1]
    for slot, position in ((0, 0), (1, ROWS + 1)):
        row_waits[slot].wait_recv()
        value = halo[slot].astype(F32)
        east = collect(east, value, position, position + 1, lanes)
        west = collect(west, value, position, position, lanes)
    edges[0] = east.astype(BF16)
    edges[1] = west.astype(BF16)
    pending.extend(row_copies)
    col_copies = cols_out(place, edges, sides, col_send, col_recv)

    bias = bias_finish(1, "x", bias_copies)
    bias_copies = bias_start(2, "y", bias)

    second_copies = []
    for a in (2, 0, 1):
        axis1, axis2, _ = ORDERS[a]
        n1, n2 = place.count[axis1], place.count[axis2]
        rows1 = HALF // n1
        rows2 = rows1 // n2
        for copy in first_copies[a]:
            copy.wait_recv()
        pending.extend(first_copies[a])
        start = pl.multiple_of(place.index[axis1] * rows1, rows1)
        total = owned[a, :, pl.ds(start, rows1), :]
        for k in range(n1 - 1):
            total = total + first_in[a][k]
        for p in range(n2):
            second_out[a][p] = total[:, p * rows2 : (p + 1) * rows2, :]
        copies = []
        for k, (device, other) in enumerate(place.peers(axis2)):
            copy = remote(second_out[a].at[other], second_in[a].at[k], sends.at[2, a, k], recvs.at[2, a, k], device)
            copy.start()
            copies.append(copy)
        second_copies.append((a, copies))

    bias = bias_finish(2, "y", bias_copies)
    bias_copies = bias_start(3, "z", bias)

    third_copies = []
    for a, copies2 in second_copies:
        _, axis2, axis3 = ORDERS[a]
        for copy in copies2:
            copy.wait_recv()
        pending.extend(copies2)
        total = second_out[a][place.index[axis2]]
        for k in range(place.count[axis2] - 1):
            total = total + second_in[a][k]
        slot = place.index[axis3]
        third[a][slot] = total
        copies = []
        for k, (device, _) in enumerate(place.peers(axis3)):
            copy = remote(third[a].at[slot], third[a].at[slot], sends.at[3, a, k], recvs.at[3, a, k], device)
            copy.start()
            copies.append(copy)
        third_copies.append((a, copies))

    bias_sum[...] = bias_finish(3, "z", bias_copies) * scaling

    fourth_copies = []
    for a, copies3 in third_copies:
        _, axis2, axis3 = ORDERS[a]
        for copy in copies3:
            copy.wait_recv()
        pending.extend(copies3)
        total = third[a][0]
        for k in range(1, place.count[axis3]):
            total = total + third[a][k]
        slot = place.index[axis2]
        gathered[a][slot] = total * scaling
        copies = []
        for k, (device, _) in enumerate(place.peers(axis2)):
            copy = remote(gathered[a].at[slot], gathered[a].at[slot], sends.at[4, a, k], recvs.at[4, a, k], device)
            copy.start()
            copies.append(copy)
        fourth_copies.append((a, copies))

    fifth_copies = []
    for a, copies4 in fourth_copies:
        axis1, axis2, _ = ORDERS[a]
        rows1 = HALF // place.count[axis1]
        for copy in copies4:
            copy.wait_recv()
        pending.extend(copies4)
        start = pl.multiple_of(mine + place.index[axis1] * rows1, rows1)
        block = kernel_sum.at[pl.ds(3 * a, 3), pl.ds(start, rows1), :]
        block[...] = jnp.concatenate([gathered[a][p] for p in range(place.count[axis2])], axis=1)
        copies = []
        for k, (device, _) in enumerate(place.peers(axis1)):
            copy = remote(block, block, sends.at[5, a, k], recvs.at[5, a, k], device)
            copy.start()
            copies.append(copy)
        fifth_copies.append((a, copies))

    last_copies = []
    for a, copies5 in fifth_copies:
        for copy in copies5:
            copy.wait_recv()
        pending.extend(copies5)
        half = kernel_sum.at[pl.ds(3 * a, 3), pl.ds(mine, HALF), :]
        copy = remote(half, half, sends.at[6, a, 0], recvs.at[6, a, 0], partner)
        copy.start()
        last_copies.append(copy)
    for copy in last_copies:
        copy.wait_recv()
    pending.extend(last_copies)
    for copy in col_copies:
        copy.wait_recv()
    pending.extend(col_copies)
    for copy in pending:
        copy.wait_send()


def field_kernel(sizes, low_rows, halo, sides, weights, grad_inputs, grad_hidden, windows, turned, wide):
    place = Place(sizes)
    width = grad_inputs.shape[0]
    lanes = lane_ids((GATES, COLS))
    low_side = sides[0].astype(F32)
    high_side = sides[1].astype(F32)
    for position in range(PADDED):
        if position == 0:
            low = halo[0]
        elif position == PADDED - 1:
            low = halo[1]
        else:
            low = low_rows[position - 1]
        before, after = spread(low.astype(F32), low_side, high_side, lanes, position)
        windows[position, 0:GATES] = before.astype(BF16)
        windows[position, GATES : 2 * GATES] = low
        windows[position, 2 * GATES : 3 * GATES] = after.astype(BF16)
    for t in range(9):
        turned[t] = jnp.transpose(weights[t].astype(F32)).astype(BF16)
    flipped = jnp.concatenate([turned[8 - q] for q in range(9)], axis=1)
    for pair in range(ROWS // 2):
        first = 2 * pair
        blocks = []
        for k in range(2):
            r = first + k
            pieces = [windows[r + d] for d in range(3)]
            if r == 0:
                pieces[0] = jnp.zeros_like(pieces[0])
            if r == ROWS - 1:
                pieces[2] = jnp.zeros_like(pieces[2])
            blocks.append(jnp.concatenate(pieces, axis=0))
        both = jnp.dot(flipped, jnp.concatenate(blocks, axis=1), preferred_element_type=F32)
        for k in range(2):
            r = first + k
            value = both[:, k * COLS : (k + 1) * COLS]
            if r == 0:
                edge = [turned[jnp.where(place.north, 2 - q, 8 - q)] for q in range(3)]
                value = value + jnp.dot(jnp.concatenate(edge, axis=1), windows[0], preferred_element_type=F32)
            if r == ROWS - 1:
                edge = [turned[jnp.where(place.south, 8 - q, 2 - q)] for q in range(3)]
                value = value + jnp.dot(
                    jnp.concatenate(edge, axis=1), windows[PADDED - 1], preferred_element_type=F32
                )
            wide[pl.ds(r, STATE, stride=ROWS), :] = value
    grad_inputs[...] = wide[pl.ds(0, width * ROWS), :].reshape(width, ROWS, COLS).astype(BF16)
    grad_hidden[...] = wide[pl.ds(width * ROWS, width * ROWS), :].reshape(width, ROWS, COLS).astype(BF16)


def shape_of(shape, dtype):
    return jax.ShapeDtypeStruct(shape, dtype)


def body(
    sizes,
    inputs_below,
    hidden_prev,
    cell_prev,
    kernel_weights,
    gate_bias,
    readout,
    target_field,
    land_mask,
    fire_mask,
    hidden_grad,
):
    nx, ny, zh, zl = sizes
    count = {"x": nx, "y": ny, "z": zh * zl}
    hid = hidden_prev.shape[0]
    dma = pltpu.SemaphoreType.DMA
    rows, sides = pl.pallas_call(
        functools.partial(halo_kernel, sizes),
        out_shape=[shape_of((PADDED, STATE, COLS), BF16), shape_of((2, STATE, COLS), BF16)],
        in_specs=[VMEM_SPEC] * 2,
        out_specs=[VMEM_SPEC] * 2,
        scratch_shapes=[
            pltpu.VMEM((STATE * ROWS, COLS), F32),
            pltpu.VMEM((2, STATE, COLS), BF16),
            pltpu.VMEM((2, STATE, COLS), BF16),
            dma((2,)),
            dma((2,)),
            dma((2,)),
            dma((2,)),
        ],
        compiler_params=pltpu.CompilerParams(
            collective_id=0, has_side_effects=True, vmem_limit_bytes=VMEM_LIMIT
        ),
        name="state_halo",
    )(inputs_below, hidden_prev)

    hidden_next, cell_next, grad_cell, kernel_part, bias_part, low_rows, low_edges = pl.pallas_call(
        local_kernel,
        out_shape=[
            shape_of((hid, ROWS, COLS), BF16),
            shape_of((hid * ROWS, COLS), F32),
            shape_of((hid * ROWS, COLS), F32),
            shape_of((9, GATES, STATE), F32),
            shape_of((8, GATES), F32),
            shape_of((ROWS, GATES, COLS), BF16),
            shape_of((2, GATES, COLS), F32),
        ],
        in_specs=[VMEM_SPEC] * 10,
        out_specs=[VMEM_SPEC] * 7,
        scratch_shapes=[
            pltpu.VMEM((PADDED, 3 * STATE, COLS), BF16),
            pltpu.VMEM((hid * ROWS, COLS), F32),
            pltpu.VMEM((hid * ROWS, COLS), F32),
        ],
        compiler_params=pltpu.CompilerParams(vmem_limit_bytes=VMEM_LIMIT),
        name="cell_step",
    )(
        rows,
        sides,
        cell_prev.reshape(hid * ROWS, COLS),
        hidden_grad,
        kernel_weights,
        gate_bias.reshape(1, GATES),
        jnp.pad(readout, (0, LANES - hid)).reshape(1, LANES),
        target_field,
        land_mask,
        fire_mask,
    )

    scaling = 1.0 / math.sqrt(ROWS * nx * zh * 2 * COLS * ny * zl)
    most = max(nx, ny, zh * zl) - 1
    chunk = []
    for axis1, axis2, axis3 in ORDERS:
        rows1 = HALF // count[axis1]
        chunk.append((count[axis1], rows1, count[axis2], rows1 // count[axis2], count[axis3]))
    kernel_sum, bias_sum, low_halo, low_sides = pl.pallas_call(
        functools.partial(reduce_kernel, sizes, scaling),
        out_shape=[
            shape_of((9, GATES, STATE), F32),
            shape_of((8, GATES), F32),
            shape_of((2, GATES, COLS), BF16),
            shape_of((2, GATES, COLS), BF16),
        ],
        in_specs=[VMEM_SPEC] * 4,
        out_specs=[VMEM_SPEC] * 4,
        scratch_shapes=[
            pltpu.VMEM((3, 3, HALF, STATE), F32),
            pltpu.VMEM((3, 3, HALF, STATE), F32),
            pltpu.VMEM((8, GATES), F32),
            pltpu.VMEM((2, GATES, COLS), BF16),
            [pltpu.VMEM((n1 - 1, 3, r1, STATE), F32) for n1, r1, _, _, _ in chunk],
            [pltpu.VMEM((n2, 3, r2, STATE), F32) for _, _, n2, r2, _ in chunk],
            [pltpu.VMEM((n2 - 1, 3, r2, STATE), F32) for _, _, n2, r2, _ in chunk],
            [pltpu.VMEM((n3, 3, r2, STATE), F32) for _, _, _, r2, n3 in chunk],
            [pltpu.VMEM((n2, 3, r2, STATE), F32) for _, _, n2, r2, _ in chunk],
            [pltpu.VMEM((n, 8, GATES), F32) for n in (2, nx, ny, zh * zl)],
            dma((2,)),
            dma((2,)),
            dma((2,)),
            dma((2,)),
            dma((7, 3, most)),
            dma((7, 3, most)),
            dma((4, most)),
            dma((4, most)),
        ],
        compiler_params=pltpu.CompilerParams(
            collective_id=1, has_side_effects=True, vmem_limit_bytes=VMEM_LIMIT
        ),
        name="kernel_reduce",
    )(kernel_part, bias_part, low_rows, low_edges)

    grad_inputs, grad_hidden = pl.pallas_call(
        functools.partial(field_kernel, sizes),
        out_shape=[shape_of((hid, ROWS, COLS), BF16)] * 2,
        in_specs=[VMEM_SPEC] * 4,
        out_specs=[VMEM_SPEC] * 2,
        scratch_shapes=[
            pltpu.VMEM((PADDED, 3 * GATES, COLS), BF16),
            pltpu.VMEM((9, STATE, GATES), BF16),
            pltpu.VMEM((STATE * ROWS, COLS), F32),
        ],
        compiler_params=pltpu.CompilerParams(vmem_limit_bytes=VMEM_LIMIT),
        name="field_gradient",
    )(low_rows, low_halo, low_sides, kernel_weights)

    shape = (hid, ROWS, COLS)
    return (
        hidden_next,
        cell_next.reshape(shape),
        grad_inputs,
        grad_hidden,
        grad_cell.reshape(shape),
        kernel_sum,
        bias_sum[0],
    )


def solution(mesh):
    lat, lon = mesh.shape["lat"], mesh.shape["lon"]
    sizes = {(16, 32): (4, 8, 2, 4), (4, 4): (2, 2, 1, 2)}[(lat, lon)]
    cells = P(None, "lat", "lon")
    flat = P("lat", "lon")
    return jax.shard_map(
        functools.partial(body, sizes),
        mesh=mesh,
        in_specs=(cells, cells, cells, P(), P(), P(), flat, flat, flat, cells),
        out_specs=(cells, cells, cells, cells, cells, P(), P()),
        check_vma=False,
    )
```

time: 487 us -> 80 us (0.16)
  waiting for transfers between devices: 253 us -> 0 us
  blocking collectives: 98.2 us -> 0 us
  Pallas kernels: 0 us -> 69.3 us
  starting transfers between devices: 58.8 us -> 0 us
  matrix products: 19.5 us -> 0 us
  local copies, waits for them, and re-layouts: 26.3 us -> 9.7 us
  other arithmetic: 16.2 us -> 0 us
  between operations: 14.6 us -> 0.69 us
    psum x1 -> x0, waiting for transfers between devices: 253 us -> none  [body(): lax.psum((local_kernel, local_bias), ('lat', 'lon'))]
    psum x1 -> x0, blocking collectives: 98.2 us -> none  [body(): lax.psum((local_kernel, local_bias), ('lat', 'lon'))]
    pallas_call x0 -> x4, Pallas kernels: none -> 69.3 us  [the longest x1 44.3 us: body(): pl.pallas_call(functools.partial(reduce_kernel, sizes, scaling), out_shap...]
    ppermute x10 -> x0, starting transfers between devices: 58.8 us -> none  [the longest x4 27.3 us: with_halo(): lax.ppermute(tail, axis, [(i, (i + 1) % count) for i in range(ends)])]
    dot_general x33 -> x0, matrix products: 19.5 us -> none  [the longest x9 8.88 us: body(): jnp.einsum('grw,crw->gc', pre_low, forward_windows[position], preferred_e...]
    dot_general x9 -> x0, local copies, waits for them, and re-layouts: 15.7 us -> none  [body(): jnp.einsum('gc,crw->grw', kernel_weights[position], forward_windows[posit...]
  transfers between devices with their start and end apart: 11 -> 0, of which waited for: 1 -> 0; matrix products, arithmetic and copies ran while one was open for 6% -> 0% of each run, Pallas kernels for 0% -> 0%
where the time goes in v1:
time: 80 us; the launch traced here: 79.6 us
  Pallas kernels  69.3 us (87%)
  local copies, waits for them, and re-layouts  9.7 us (12%)
    pallas_call x1, Pallas kernels, body(): pl.pallas_call(functools.partial(reduce_kernel, sizes, scaling), out_shap...  44.3 us
    pallas_call x1, Pallas kernels, body(): pl.pallas_call(functools.partial(halo_kernel, sizes), out_shape=[shape_of...  20.4 us
    unnamed x21, local copies, waits for them, and re-layouts  8.48 us
    pallas_call x1, Pallas kernels, body(): pl.pallas_call(local_kernel, out_shape=[shape_of((hid, ROWS, COLS), BF16)...  2.59 us
    pallas_call x1, Pallas kernels, body(): pl.pallas_call(functools.partial(field_kernel, sizes), out_shape=[shape_o...  2.03 us

profile of v1, /device:TPU:1, one launch (start us, length us, event | category | flops | bytes accessed | tf_op | source)
XLA Modules:
  0.0 79.6 jit_solution(10012569975398506253)
XLA Ops:
  0.6 0.7 pad_bitcast_fusion.readout
  1.3 0.0 copy-start.4
  1.3 0.9 %copy-done.4 = bf16[64,8,128]{2,1,0:T(8,128)(2,1)S(1)} copy-done((bf16[64,8,128]{2,1,0:T(8,128)(2,1)S(1)}, bf16[64,8,128]{2,1,0:T(8,128)(2,1)}, u32[]{:S(2)}) %copy-start.4) | copy-done | bytes 131096
  2.2 0.0 copy-start.5
  2.2 0.9 %copy-done.5 = bf16[64,8,128]{2,1,0:T(8,128)(2,1)S(1)} copy-done((bf16[64,8,128]{2,1,0:T(8,128)(2,1)S(1)}, bf16[64,8,128]{2,1,0:T(8,128)(2,1)}, u32[]{:S(2)}) %copy-start.5) | copy-done | bytes 131096
  3.1 20.4 %state_halo.1 = (bf16[10,128,128]{2,1,0:T(8,128)(2,1)S(1)}, bf16[2,128,128]{2,1,0:T(8,128)(2,1)S(1)}) custom-call(bf16[64,8,128]{2,1,0:T(8,128)(2,1)S(1)} %copy-done.4, bf16[64,8,128]{2,1,0:T(8,128)(2,1)S(1)} %copy-done.5), custom_call_target="tpu_custom_call" | custom-call | tf_op jit(solution)/shard_map/state_halo/pallas_call | solution.py:564
  23.5 0.0 copy-start
  23.5 1.1 %copy-done = bf16[9,256,128]{2,1,0:T(8,128)(2,1)S(1)} copy-done((bf16[9,256,128]{2,1,0:T(8,128)(2,1)S(1)}, bf16[9,256,128]{2,1,0:T(8,128)(2,1)}, u32[]{:S(2)}) %copy-start) | copy-done | bytes 589848
  24.5 0.0 copy-start.2
  24.5 0.9 %copy-done.2 = f32[64,8,128]{2,1,0:T(8,128)S(1)} copy-done((f32[64,8,128]{2,1,0:T(8,128)S(1)}, f32[64,8,128]{2,1,0:T(8,128)}, u32[]{:S(2)}) %copy-start.2) | copy-done | bytes 262168
  25.5 0.0 copy-start.3
  25.5 0.9 %copy-done.3 = bf16[64,8,128]{2,1,0:T(8,128)(2,1)S(1)} copy-done((bf16[64,8,128]{2,1,0:T(8,128)(2,1)S(1)}, bf16[64,8,128]{2,1,0:T(8,128)(2,1)}, u32[]{:S(2)}) %copy-start.3) | copy-done | bytes 131096
  26.4 0.0 copy-start.6
  26.4 0.7 copy-done.6
  27.1 0.0 copy-start.7
  27.1 0.7 copy-done.7
  27.8 0.0 copy-start.8
  27.8 0.7 copy-done.8
  28.5 0.0 copy-start.9
  28.5 0.7 copy-done.9
  29.1 2.6 %cell_step.1 = (bf16[64,8,128]{2,1,0:T(8,128)(2,1)}, f32[512,128]{1,0:T(8,128)}, f32[512,128]{1,0:T(8,128)}, f32[9,256,128]{2,1,0:T(8,128)S(1)}, f32[8,256]{1,0:...) custom-call(bf16[10,128,128]{2,1,0:T(8,128)(2,1)S(1)} %get-tuple-element.22.rows, ...), custom_call_target="tpu_custom_call" | custom-call | tf_op jit(solution)/shard_map/cell_step/pallas_call | solution.py:584
  31.7 0.0 copy-start.1
  31.7 44.3 %kernel_reduce.1 = (f32[9,256,128]{2,1,0:T(8,128)S(1)}, f32[8,256]{1,0:T(8,128)S(1)}, bf16[2,256,128]{2,1,0:T(8,128)(2,1)S(1)}, bf16[2,256,128]{2,1,0:T(8,128)(2,1)S(1)}) custom-call(f32[9,256,128]{2,1,0:T(8,128)S(1)} %get-tuple-element.27.kernel_part, f32[8,256]{1,0:T(8,128)S(1)} %get-tuple-element.28.bias_part, ...), custom_call_target="tpu_custom_call" | custom-call | tf_op jit(solution)/shard_map/kernel_reduce/pallas_call | solution.py:623
  76.0 0.0 copy-done.1
  76.0 2.0 %field_gradient.1 = (bf16[64,8,128]{2,1,0:T(8,128)(2,1)}, bf16[64,8,128]{2,1,0:T(8,128)(2,1)}) custom-call(bf16[8,256,128]{2,1,0:T(8,128)(2,1)S(1)} %get-tuple-element.26.low_rows, bf16[2,256,128]{2,1,0:T(8,128)(2,1)S(1)} %get-tuple-element.30.halo, bf16[2,256,128]{2,1,0:T(8,128)(2,1)S(1)} %get-tuple-element.31.sides, bf16[9,256,128]{2,1,0:T(8,128)(2,1)S(1)} %copy-done.1), custom_call_target="tpu_custom_call" | custom-call | tf_op jit(solution)/shard_map/field_gradient/pallas_call | solution.py:659
  78.1 0.6 slice.3
  78.6 1.0 %copy.18 = f32[9,256,128]{2,1,0:T(8,128)} copy(f32[9,256,128]{2,1,0:T(8,128)S(1)} %get-tuple-element.49) | data formatting | bytes 2359296
Async XLA Ops:
  1.3 0.9 %copy-start.4 = (bf16[64,8,128]{2,1,0:T(8,128)(2,1)S(1)}, bf16[64,8,128]{2,1,0:T(8,128)(2,1)}, u32[]{:S(2)}) copy-start(bf16[64,8,128]{2,1,0:T(8,128)(2,1)} %below.1) | copy-start | bytes 393220
  2.2 0.9 %copy-start.5 = (bf16[64,8,128]{2,1,0:T(8,128)(2,1)S(1)}, bf16[64,8,128]{2,1,0:T(8,128)(2,1)}, u32[]{:S(2)}) copy-start(bf16[64,8,128]{2,1,0:T(8,128)(2,1)} %hidden.1) | copy-start | bytes 393220
  23.5 1.1 %copy-start = (bf16[9,256,128]{2,1,0:T(8,128)(2,1)S(1)}, bf16[9,256,128]{2,1,0:T(8,128)(2,1)}, u32[]{:S(2)}) copy-start(bf16[9,256,128]{2,1,0:T(8,128)(2,1)} %weights.3) | copy-start | bytes 1769476
  24.5 0.9 %copy-start.2 = (f32[64,8,128]{2,1,0:T(8,128)S(1)}, f32[64,8,128]{2,1,0:T(8,128)}, u32[]{:S(2)}) copy-start(f32[64,8,128]{2,1,0:T(8,128)} %param.12) | copy-start | bytes 786436
  25.5 0.9 %copy-start.3 = (bf16[64,8,128]{2,1,0:T(8,128)(2,1)S(1)}, bf16[64,8,128]{2,1,0:T(8,128)(2,1)}, u32[]{:S(2)}) copy-start(bf16[64,8,128]{2,1,0:T(8,128)(2,1)} %hidden_grad.1) | copy-start | bytes 393220
  26.4 0.7 copy-start.6
  27.1 0.7 copy-start.7
  27.8 0.7 copy-start.8
  28.5 0.7 copy-start.9
  31.7 44.3 %copy-start.1 = (bf16[9,256,128]{2,1,0:T(8,128)(2,1)S(1)}, bf16[9,256,128]{2,1,0:T(8,128)(2,1)}, u32[]{:S(2)}) copy-start(bf16[9,256,128]{2,1,0:T(8,128)(2,1)} %weights.3) | copy-start | bytes 1769476

commit v2 on v1

v2 whole, which is shorter than its diff:
```python
import functools
import math

import jax
import jax.numpy as jnp
from jax import lax
from jax.experimental import pallas as pl
from jax.experimental.pallas import tpu as pltpu
from jax.sharding import PartitionSpec as P

MESH = pl.DeviceIdType.MESH
F32 = jnp.float32
BF16 = jnp.bfloat16
ROWS = 8
COLS = 128
PADDED = ROWS + 2
STATE = 128
GATES = 256
HALF = GATES // 2
LANES = 128
VMEM_SPEC = pl.BlockSpec(memory_space=pltpu.VMEM)
VMEM_LIMIT = 48 * 1024 * 1024


class Place:
    def __init__(self, sizes):
        self.nx, self.ny, self.zh, self.zl = sizes
        self.nz = self.zh * self.zl
        self.nlat = self.nx * self.zh * 2
        self.nlon = self.ny * self.zl
        self.lat = lax.axis_index("lat")
        self.lon = lax.axis_index("lon")
        self.core = lax.rem(self.lat, 2)
        chip = self.lat // 2
        self.z_hi = lax.rem(chip, self.zh)
        self.x = chip // self.zh
        self.z_lo = lax.rem(self.lon, self.zl)
        self.y = self.lon // self.zl
        self.z = self.z_hi * self.zl + self.z_lo
        self.count = {"core": 2, "x": self.nx, "y": self.ny, "z": self.nz}
        self.index = {"core": self.core, "x": self.x, "y": self.y, "z": self.z}
        self.north = self.lat == 0
        self.south = self.lat == self.nlat - 1

    def at(self, x, y, z, core):
        lat = (x * self.zh + z // self.zl) * 2 + core
        lon = y * self.zl + lax.rem(z, self.zl)
        return (lat, lon)

    def peer(self, axis, steps):
        other = lax.rem(self.index[axis] + steps, self.count[axis])
        where = dict(self.index)
        where[axis] = other
        return self.at(where["x"], where["y"], where["z"], where["core"]), other

    def peers(self, axis):
        count = self.count[axis]
        order = sorted(range(1, count), key=lambda steps: min(steps, count - steps))
        return [(steps - 1, *self.peer(axis, steps)) for steps in order]

    def up(self):
        opposite = lax.rem(self.lon + self.nlon // 2, self.nlon)
        lat = jnp.where(self.north, 0, self.lat - 1)
        return (lat, jnp.where(self.north, opposite, self.lon))

    def down(self):
        opposite = lax.rem(self.lon + self.nlon // 2, self.nlon)
        lat = jnp.where(self.south, self.nlat - 1, self.lat + 1)
        return (lat, jnp.where(self.south, opposite, self.lon))

    def east(self):
        return (self.lat, lax.rem(self.lon + 1, self.nlon))

    def west(self):
        return (self.lat, lax.rem(self.lon + self.nlon - 1, self.nlon))

    def around(self):
        return [self.up(), self.down(), self.east(), self.west()]


def greet(devices):
    barrier = pltpu.get_barrier_semaphore()
    for device in devices:
        pl.semaphore_signal(barrier, inc=1, device_id=device, device_id_type=MESH)
    return barrier


def remote(source, target, send_sem, recv_sem, device):
    return pltpu.make_async_remote_copy(
        src_ref=source,
        dst_ref=target,
        send_sem=send_sem,
        recv_sem=recv_sem,
        device_id=device,
        device_id_type=MESH,
    )


def lane_ids(shape):
    return lax.broadcasted_iota(jnp.int32, shape, len(shape) - 1)


def rows_out(place, first, last, halo, send_sem, recv_sem):
    upper_slot = jnp.where(place.north, 0, 1)
    lower_slot = jnp.where(place.south, 1, 0)
    copies = [
        remote(first, halo.at[upper_slot], send_sem.at[0], recv_sem.at[upper_slot], place.up()),
        remote(last, halo.at[lower_slot], send_sem.at[1], recv_sem.at[lower_slot], place.down()),
    ]
    for copy in copies:
        copy.start()
    waits = [
        remote(first, halo.at[0], send_sem.at[0], recv_sem.at[0], place.up()),
        remote(last, halo.at[1], send_sem.at[1], recv_sem.at[1], place.down()),
    ]
    return copies, waits


def collect(total, row, position, shift, lanes):
    return jnp.where(lanes == position, pltpu.roll(row, shift % LANES, 1), total)


def cols_out(place, edges, sides, send_sem, recv_sem):
    copies = [
        remote(edges.at[0], sides.at[0], send_sem.at[0], recv_sem.at[0], place.east()),
        remote(edges.at[1], sides.at[1], send_sem.at[1], recv_sem.at[1], place.west()),
    ]
    for copy in copies:
        copy.start()
    return copies


def spread(values, sides_low, sides_high, lanes, position):
    before = jnp.where(lanes == 0, pltpu.roll(sides_low, (-position) % LANES, 1), pltpu.roll(values, 1, 1))
    after = jnp.where(
        lanes == COLS - 1, pltpu.roll(sides_high, (COLS - 1 - position) % LANES, 1), pltpu.roll(values, COLS - 1, 1)
    )
    return before, after


ORDERS = (("y", "x", "z"), ("z", "x", "y"), ("x", "y", "z"))
EARLY = ((1, 2), (3, 4), (5, 6))
LATE = (0, 7)


def step_kernel(
    sizes,
    scaling,
    below_hbm,
    hidden_hbm,
    cell_hbm,
    weights_hbm,
    gate_bias_hbm,
    readout_hbm,
    target_hbm,
    land_hbm,
    fire_hbm,
    hidden_grad_hbm,
    hidden_next,
    cell_next,
    grad_inputs,
    grad_hidden,
    grad_cell,
    kernel_low,
    bias_sum,
    below,
    hidden,
    cell_prev,
    weights,
    gate_bias,
    readout,
    target,
    land,
    fire,
    hidden_grad,
    wide,
    wide_grad,
    rows,
    halo,
    edges,
    sides,
    corner_edges,
    corners,
    windows,
    kernel_acc,
    turned,
    low_rows,
    low_halo,
    low_edges,
    low_sides,
    low_windows,
    pair_out,
    pair_in,
    owned,
    first_out,
    first_in,
    second_out,
    second_in,
    third,
    gathered,
    bias_bufs,
    load_sem,
    row_send,
    row_recv,
    col_send,
    col_recv,
    sends,
    recvs,
    bias_send,
    bias_recv,
):
    place = Place(sizes)
    hid = hidden_next.shape[0]
    width = grad_inputs.shape[0]
    partner, _ = place.peer("core", 1)
    devices = [partner] + place.around()
    for axis in ("x", "y", "z"):
        devices += [device for _, device, _ in place.peers(axis)]
    barrier = greet(devices)
    mine = pl.multiple_of(place.core * HALF, HALF)
    theirs = pl.multiple_of((1 - place.core) * HALF, HALF)
    pending = []

    sources = (below_hbm, hidden_hbm, weights_hbm, cell_hbm, hidden_grad_hbm, gate_bias_hbm, readout_hbm,
               target_hbm, land_hbm, fire_hbm)
    targets = (below, hidden, weights, cell_prev, hidden_grad, gate_bias, readout, target, land, fire)
    loads = [
        pltpu.make_async_copy(source, destination, load_sem.at[i])
        for i, (source, destination) in enumerate(zip(sources, targets))
    ]
    for load in loads:
        load.start()

    loads[0].wait()
    wide[pl.ds(0, width * ROWS), :] = below[...].astype(F32).reshape(width * ROWS, COLS)
    loads[1].wait()
    wide[pl.ds(width * ROWS, hid * ROWS), :] = hidden[...].astype(F32).reshape(hid * ROWS, COLS)

    def state_row(r):
        return wide[pl.ds(r, STATE, stride=ROWS), :]

    lanes = lane_ids((STATE, COLS))
    east = jnp.zeros((STATE, COLS), F32)
    west = jnp.zeros((STATE, COLS), F32)
    for r in range(ROWS):
        value = state_row(r)
        rows[r + 1] = value.astype(BF16)
        east = collect(east, value, r + 1, r + 2, lanes)
        west = collect(west, value, r + 1, r + 1, lanes)
    edges[0] = east.astype(BF16)
    edges[1] = west.astype(BF16)
    for load in loads[2:]:
        load.wait()
    for t in range(9):
        turned[t] = jnp.transpose(weights[t].astype(F32)).astype(BF16)
    wide_grad[...] = hidden_grad[...].astype(F32).reshape(hid * ROWS, COLS)
    bias_cols = jnp.transpose(jnp.broadcast_to(gate_bias[...], (LANES, GATES)))
    read_cols = jnp.transpose(jnp.broadcast_to(readout[...], (LANES, hid)))

    pl.semaphore_wait(barrier, len(devices))
    row_copies, row_waits = rows_out(place, rows.at[1], rows.at[ROWS], halo, row_send.at[0], row_recv.at[0])
    col_copies = cols_out(place, edges, sides, col_send.at[0], col_recv.at[0])

    corner_east = jnp.zeros((STATE, COLS), F32)
    corner_west = jnp.zeros((STATE, COLS), F32)
    for slot, position in ((0, 0), (1, PADDED - 1)):
        row_waits[slot].wait_recv()
        value = halo[slot].astype(F32)
        corner_east = collect(corner_east, value, position, position + 1, lanes)
        corner_west = collect(corner_west, value, position, position, lanes)
    corner_edges[0] = corner_east.astype(BF16)
    corner_edges[1] = corner_west.astype(BF16)
    corner_copies = cols_out(place, corner_edges, corners, col_send.at[1], col_recv.at[1])
    pending += row_copies + col_copies + corner_copies

    def open_windows(position, low, side_refs):
        value = low.astype(F32)
        before, after = spread(value, side_refs[0].astype(F32), side_refs[1].astype(F32), lanes, position)
        windows[position, 0:STATE] = before.astype(BF16)
        windows[position, STATE : 2 * STATE] = low
        windows[position, 2 * STATE : 3 * STATE] = after.astype(BF16)

    for copy in col_copies:
        copy.wait_recv()
    for position in range(1, PADDED - 1):
        open_windows(position, rows[position], sides)

    flat = jnp.concatenate([weights[t] for t in range(9)], axis=1)

    def cells_of(pair, bias_total):
        columns = jnp.concatenate([windows[r : r + 3].reshape(9 * STATE, COLS) for r in pair], axis=1)
        both = jnp.dot(flat, columns, preferred_element_type=F32)
        for k, r in enumerate(pair):
            preact = both[:, k * COLS : (k + 1) * COLS] + bias_cols
            input_gate = jax.nn.sigmoid(preact[0:hid])
            forget_gate = jax.nn.sigmoid(preact[hid : 2 * hid])
            output_gate = jax.nn.sigmoid(preact[2 * hid : 3 * hid])
            candidate = jnp.tanh(preact[3 * hid : 4 * hid])
            land_row = land[r : r + 1, :].astype(F32)
            fire_row = fire[r : r + 1, :].astype(F32)
            prev = cell_prev[pl.ds(r, hid, stride=ROWS), :]
            cell = land_row * (forget_gate * prev + input_gate * candidate)
            squashed = jnp.tanh(cell)
            new_hidden = (output_gate * squashed).astype(BF16).astype(F32)
            predicted = jnp.sum(read_cols * new_hidden, axis=0, keepdims=True)
            miss = 2.0 * (fire_row * (predicted - target[r : r + 1, :]))
            total_grad = wide_grad[pl.ds(r, hid, stride=ROWS), :] + miss * read_cols
            cell_grad = land_row * total_grad * output_gate * (1.0 - squashed * squashed)
            pre_grad = jnp.concatenate(
                [
                    cell_grad * candidate * input_gate * (1.0 - input_gate),
                    cell_grad * prev * forget_gate * (1.0 - forget_gate),
                    total_grad * squashed * output_gate * (1.0 - output_gate),
                    cell_grad * input_gate * (1.0 - candidate * candidate),
                ],
                axis=0,
            )
            cell_next[pl.ds(r, hid, stride=ROWS), :] = cell
            grad_cell[pl.ds(r, hid, stride=ROWS), :] = cell_grad * forget_gate
            wide[pl.ds(r, hid, stride=ROWS), :] = new_hidden
            bias_total = bias_total + pre_grad
            low_rows[r] = pre_grad.astype(BF16)
        return bias_total

    def kernel_terms(gates, rows_in, a):
        cells = jnp.concatenate([low_rows[r, gates, :] for r in rows_in], axis=1)
        seen = jnp.concatenate([windows[r + a] for r in rows_in], axis=1)
        return lax.dot_general(cells, seen, (((1,), (1,)), ((), ())), preferred_element_type=F32)

    bias_total = jnp.zeros((GATES, COLS), F32)
    for pair in EARLY:
        bias_total = cells_of(pair, bias_total)
    for a in range(3):
        kernel_acc[a] = kernel_terms(slice(None), range(1, ROWS - 1), a)

    for copy in corner_copies:
        copy.wait_recv()
    open_windows(0, halo[0], corners)
    open_windows(PADDED - 1, halo[1], corners)
    bias_total = cells_of(LATE, bias_total)

    pair_copies = []
    for a in range(3):
        part = kernel_acc[a, pl.ds(theirs, HALF), :] + kernel_terms(pl.ds(theirs, HALF), LATE, a)
        for b in range(3):
            pair_out[a, b] = part[:, b * STATE : (b + 1) * STATE].astype(BF16)
        copy = remote(pair_out.at[a], pair_in.at[a], sends.at[0, a, 0], recvs.at[0, a, 0], partner)
        copy.start()
        pair_copies.append(copy)
    for a in range(3):
        part = kernel_acc[a, pl.ds(mine, HALF), :] + kernel_terms(pl.ds(mine, HALF), LATE, a)
        for b in range(3):
            owned[a, b] = part[:, b * STATE : (b + 1) * STATE]

    first_copies = []
    for a in range(3):
        pair_copies[a].wait_recv()
        total = owned[a] + pair_in[a].astype(F32)
        owned[a] = total
        first_out[a] = total.astype(BF16)
        axis = ORDERS[a][0]
        rows1 = HALF // place.count[axis]
        copies = []
        for k, device, other in reversed(place.peers(axis)):
            start = pl.multiple_of(other * rows1, rows1)
            copy = remote(
                first_out.at[a, :, pl.ds(start, rows1), :],
                first_in[a].at[k],
                sends.at[1, a, k],
                recvs.at[1, a, k],
                device,
            )
            copy.start()
            copies.append(copy)
        first_copies.append(copies)
    pending += pair_copies

    def bias_start(stage, axis, value):
        slot = place.index[axis]
        buf = bias_bufs[stage]
        buf[slot] = value
        copies = []
        for k, device, _ in place.peers(axis):
            copy = remote(buf.at[slot], buf.at[slot], bias_send.at[stage, k], bias_recv.at[stage, k], device)
            copy.start()
            copies.append(copy)
        return copies

    def bias_finish(stage, axis, copies):
        buf = bias_bufs[stage]
        for copy in copies:
            copy.wait_recv()
        pending.extend(copies)
        total = buf[0]
        for k in range(1, place.count[axis]):
            total = total + buf[k]
        return total

    bias = lax.dot_general(
        jnp.ones((8, COLS), F32),
        bias_total,
        (((1,), (1,)), ((), ())),
        precision=lax.Precision.HIGHEST,
        preferred_element_type=F32,
    )
    bias_copies = bias_start(0, "core", bias)
    row_copies, row_waits = rows_out(
        place, low_rows.at[0], low_rows.at[ROWS - 1], low_halo, row_send.at[1], row_recv.at[1]
    )
    hidden_next[...] = wide[pl.ds(0, hid * ROWS), :].reshape(hid, ROWS, COLS).astype(BF16)
    gate_lanes = lane_ids((GATES, COLS))
    east = jnp.zeros((GATES, COLS), F32)
    west = jnp.zeros((GATES, COLS), F32)
    for r in range(ROWS):
        value = low_rows[r].astype(F32)
        east = collect(east, value, r + 1, r + 2, gate_lanes)
        west = collect(west, value, r + 1, r + 1, gate_lanes)
    bias = bias_finish(0, "core", bias_copies)
    bias_copies = bias_start(1, "x", bias)
    for slot, position in ((0, 0), (1, PADDED - 1)):
        row_waits[slot].wait_recv()
        value = low_halo[slot].astype(F32)
        east = collect(east, value, position, position + 1, gate_lanes)
        west = collect(west, value, position, position, gate_lanes)
    low_edges[0] = east.astype(BF16)
    low_edges[1] = west.astype(BF16)
    low_copies = cols_out(place, low_edges, low_sides, col_send.at[2], col_recv.at[2])
    pending += row_copies + low_copies
    bias = bias_finish(1, "x", bias_copies)
    bias_copies = bias_start(2, "y", bias)

    second_copies = []
    for a in (2, 0, 1):
        axis1, axis2, _ = ORDERS[a]
        n1, n2 = place.count[axis1], place.count[axis2]
        rows1 = HALF // n1
        rows2 = rows1 // n2
        for copy in reversed(first_copies[a]):
            copy.wait_recv()
        pending += first_copies[a]
        start = pl.multiple_of(place.index[axis1] * rows1, rows1)
        total = owned[a, :, pl.ds(start, rows1), :]
        for k in range(n1 - 1):
            total = total + first_in[a][k].astype(F32)
        for p in range(n2):
            second_out[a][p] = total[:, p * rows2 : (p + 1) * rows2, :]
        copies = []
        for k, device, other in reversed(place.peers(axis2)):
            copy = remote(second_out[a].at[other], second_in[a].at[k], sends.at[2, a, k], recvs.at[2, a, k], device)
            copy.start()
            copies.append(copy)
        second_copies.append((a, copies))

    bias = bias_finish(2, "y", bias_copies)
    bias_copies = bias_start(3, "z", bias)

    third_copies = []
    for a, copies2 in second_copies:
        _, axis2, axis3 = ORDERS[a]
        for copy in reversed(copies2):
            copy.wait_recv()
        pending += copies2
        total = second_out[a][place.index[axis2]]
        for k in range(place.count[axis2] - 1):
            total = total + second_in[a][k]
        slot = place.index[axis3]
        third[a][slot] = total
        copies = []
        for k, device, _ in reversed(place.peers(axis3)):
            copy = remote(third[a].at[slot], third[a].at[slot], sends.at[3, a, k], recvs.at[3, a, k], device)
            copy.start()
            copies.append(copy)
        third_copies.append((a, copies))

    bias_sum[...] = bias_finish(3, "z", bias_copies) * scaling

    fourth_copies = []
    for a, copies3 in third_copies:
        _, axis2, axis3 = ORDERS[a]
        for copy in reversed(copies3):
            copy.wait_recv()
        pending += copies3
        total = third[a][0]
        for k in range(1, place.count[axis3]):
            total = total + third[a][k]
        slot = place.index[axis2]
        gathered[a][slot] = total * scaling
        copies = []
        for k, device, _ in reversed(place.peers(axis2)):
            copy = remote(gathered[a].at[slot], gathered[a].at[slot], sends.at[4, a, k], recvs.at[4, a, k], device)
            copy.start()
            copies.append(copy)
        fourth_copies.append((a, copies))

    def block_of(a, owner):
        rows1 = HALF // place.count[ORDERS[a][0]]
        start = pl.multiple_of(mine + owner * rows1, rows1)
        return kernel_low.at[pl.ds(3 * a, 3), pl.ds(start, rows1), :]

    last_copies = []

    def forward(a, owner, slot):
        block = block_of(a, owner)
        copy = remote(block, block, sends.at[6, a, slot], recvs.at[6, a, slot], partner)
        copy.start()
        last_copies.append(copy)

    fifth_copies = []
    for a, copies4 in fourth_copies:
        axis1, axis2, _ = ORDERS[a]
        n1 = place.count[axis1]
        for copy in reversed(copies4):
            copy.wait_recv()
        pending += copies4
        block = block_of(a, place.index[axis1])
        block[...] = jnp.concatenate([gathered[a][p] for p in range(place.count[axis2])], axis=1).astype(BF16)
        copies = []
        for k, device, _ in reversed(place.peers(axis1)):
            copy = remote(block, block, sends.at[5, a, k], recvs.at[5, a, k], device)
            copy.start()
            copies.append((copy, k, lax.rem(place.index[axis1] + n1 - 1 - k, n1)))
        forward(a, place.index[axis1], n1 - 1)
        fifth_copies.append((a, copies))

    for copy in low_copies:
        copy.wait_recv()
    low_side = low_sides[0].astype(F32)
    high_side = low_sides[1].astype(F32)
    for position in range(PADDED):
        if position == 0:
            low = low_halo[0]
        elif position == PADDED - 1:
            low = low_halo[1]
        else:
            low = low_rows[position - 1]
        before, after = spread(low.astype(F32), low_side, high_side, gate_lanes, position)
        low_windows[position, 0:GATES] = before.astype(BF16)
        low_windows[position, GATES : 2 * GATES] = low
        low_windows[position, 2 * GATES : 3 * GATES] = after.astype(BF16)
    flipped = jnp.concatenate([turned[8 - q] for q in range(9)], axis=1)
    for pair in range(ROWS // 2):
        first = 2 * pair
        blocks = []
        for k in range(2):
            r = first + k
            pieces = [low_windows[r + d] for d in range(3)]
            if r == 0:
                pieces[0] = jnp.zeros_like(pieces[0])
            if r == ROWS - 1:
                pieces[2] = jnp.zeros_like(pieces[2])
            blocks.append(jnp.concatenate(pieces, axis=0))
        both = jnp.dot(flipped, jnp.concatenate(blocks, axis=1), preferred_element_type=F32)
        for k in range(2):
            r = first + k
            value = both[:, k * COLS : (k + 1) * COLS]
            if r == 0:
                edge = [turned[jnp.where(place.north, 2 - q, 8 - q)] for q in range(3)]
                value = value + jnp.dot(jnp.concatenate(edge, axis=1), low_windows[0], preferred_element_type=F32)
            if r == ROWS - 1:
                edge = [turned[jnp.where(place.south, 8 - q, 2 - q)] for q in range(3)]
                value = value + jnp.dot(
                    jnp.concatenate(edge, axis=1), low_windows[PADDED - 1], preferred_element_type=F32
                )
            wide[pl.ds(r, STATE, stride=ROWS), :] = value
    grad_inputs[...] = wide[pl.ds(0, width * ROWS), :].reshape(width, ROWS, COLS).astype(BF16)
    grad_hidden[...] = wide[pl.ds(width * ROWS, hid * ROWS), :].reshape(hid, ROWS, COLS).astype(BF16)

    for a, copies5 in fifth_copies:
        for copy, k, sender in reversed(copies5):
            copy.wait_recv()
            forward(a, sender, k)
            pending.append(copy)
    for copy in last_copies:
        copy.wait_recv()
    pending += last_copies
    for copy in pending:
        copy.wait_send()


def finish_kernel(
    hidden_next,
    cell_next,
    grad_inputs,
    grad_hidden,
    grad_cell,
    kernel_low,
    bias_sum,
    hidden_next_out,
    cell_next_out,
    grad_inputs_out,
    grad_hidden_out,
    grad_cell_out,
    kernel_out,
    bias_out,
    kernel_wide,
    sems,
):
    pairs = (
        (hidden_next, hidden_next_out),
        (cell_next, cell_next_out),
        (grad_inputs, grad_inputs_out),
        (grad_hidden, grad_hidden_out),
        (grad_cell, grad_cell_out),
        (bias_sum.at[0:1], bias_out),
    )
    copies = [pltpu.make_async_copy(source, target, sems.at[i]) for i, (source, target) in enumerate(pairs)]
    for copy in copies:
        copy.start()
    for a in range(3):
        taps = pl.ds(3 * a, 3)
        kernel_wide[taps] = kernel_low[taps].astype(F32)
        copy = pltpu.make_async_copy(kernel_wide.at[taps], kernel_out.at[taps], sems.at[len(pairs) + a])
        copy.start()
        copies.append(copy)
    for copy in copies:
        copy.wait()


def shape_of(shape, dtype):
    return jax.ShapeDtypeStruct(shape, dtype)


def body(
    sizes,
    inputs_below,
    hidden_prev,
    cell_prev,
    kernel_weights,
    gate_bias,
    readout,
    target_field,
    land_mask,
    fire_mask,
    hidden_grad,
):
    nx, ny, zh, zl = sizes
    count = {"x": nx, "y": ny, "z": zh * zl}
    hid = hidden_prev.shape[0]
    dma = pltpu.SemaphoreType.DMA
    scaling = 1.0 / math.sqrt(ROWS * nx * zh * 2 * COLS * ny * zl)
    most = max(nx, ny, zh * zl)
    chunk = []
    for axis1, axis2, axis3 in ORDERS:
        rows1 = HALF // count[axis1]
        chunk.append((count[axis1], rows1, count[axis2], rows1 // count[axis2], count[axis3]))
    cells = shape_of((hid, ROWS, COLS), BF16)
    wide_cells = shape_of((hid * ROWS, COLS), F32)
    inputs = (
        inputs_below,
        hidden_prev,
        cell_prev.reshape(hid * ROWS, COLS),
        kernel_weights,
        gate_bias.reshape(1, GATES),
        readout.reshape(1, hid),
        target_field,
        land_mask,
        fire_mask,
        hidden_grad,
    )
    results = pl.pallas_call(
        functools.partial(step_kernel, sizes, scaling),
        out_shape=[
            cells,
            wide_cells,
            cells,
            cells,
            wide_cells,
            shape_of((9, GATES, STATE), BF16),
            shape_of((8, GATES), F32),
        ],
        in_specs=[pl.BlockSpec(memory_space=pltpu.HBM)] * len(inputs),
        out_specs=[VMEM_SPEC] * 7,
        scratch_shapes=[pltpu.VMEM(value.shape, value.dtype) for value in inputs]
        + [
            pltpu.VMEM((STATE * ROWS, COLS), F32),
            pltpu.VMEM((hid * ROWS, COLS), F32),
            pltpu.VMEM((PADDED, STATE, COLS), BF16),
            pltpu.VMEM((2, STATE, COLS), BF16),
            pltpu.VMEM((2, STATE, COLS), BF16),
            pltpu.VMEM((2, STATE, COLS), BF16),
            pltpu.VMEM((2, STATE, COLS), BF16),
            pltpu.VMEM((2, STATE, COLS), BF16),
            pltpu.VMEM((PADDED, 3 * STATE, COLS), BF16),
            pltpu.VMEM((3, GATES, 3 * STATE), F32),
            pltpu.VMEM((9, STATE, GATES), BF16),
            pltpu.VMEM((ROWS, GATES, COLS), BF16),
            pltpu.VMEM((2, GATES, COLS), BF16),
            pltpu.VMEM((2, GATES, COLS), BF16),
            pltpu.VMEM((2, GATES, COLS), BF16),
            pltpu.VMEM((PADDED, 3 * GATES, COLS), BF16),
            pltpu.VMEM((3, 3, HALF, STATE), BF16),
            pltpu.VMEM((3, 3, HALF, STATE), BF16),
            pltpu.VMEM((3, 3, HALF, STATE), F32),
            pltpu.VMEM((3, 3, HALF, STATE), BF16),
            [pltpu.VMEM((n1 - 1, 3, r1, STATE), BF16) for n1, r1, _, _, _ in chunk],
            [pltpu.VMEM((n2, 3, r2, STATE), F32) for _, _, n2, r2, _ in chunk],
            [pltpu.VMEM((n2 - 1, 3, r2, STATE), F32) for _, _, n2, r2, _ in chunk],
            [pltpu.VMEM((n3, 3, r2, STATE), F32) for _, _, _, r2, n3 in chunk],
            [pltpu.VMEM((n2, 3, r2, STATE), F32) for _, _, n2, r2, _ in chunk],
            [pltpu.VMEM((n, 8, GATES), F32) for n in (2, nx, ny, zh * zl)],
            dma((len(inputs),)),
            dma((2, 2)),
            dma((2, 2)),
            dma((3, 2)),
            dma((3, 2)),
            dma((7, 3, most)),
            dma((7, 3, most)),
            dma((4, most)),
            dma((4, most)),
        ],
        compiler_params=pltpu.CompilerParams(
            collective_id=0, has_side_effects=True, vmem_limit_bytes=VMEM_LIMIT
        ),
        name="whole_step",
    )(*[pltpu.with_memory_space_constraint(value, pltpu.HBM) for value in inputs])

    hidden_next, cell_next, grad_inputs, grad_hidden, grad_cell, grad_kernel, grad_bias = pl.pallas_call(
        finish_kernel,
        out_shape=[
            cells,
            wide_cells,
            cells,
            cells,
            wide_cells,
            shape_of((9, GATES, STATE), F32),
            shape_of((1, GATES), F32),
        ],
        in_specs=[VMEM_SPEC] * 7,
        out_specs=[pl.BlockSpec(memory_space=pltpu.HBM)] * 7,
        scratch_shapes=[pltpu.VMEM((9, GATES, STATE), F32), dma((9,))],
        compiler_params=pltpu.CompilerParams(vmem_limit_bytes=VMEM_LIMIT),
        name="results",
    )(*results)
    shape = (hid, ROWS, COLS)
    return (
        hidden_next,
        cell_next.reshape(shape),
        grad_inputs,
        grad_hidden,
        grad_cell.reshape(shape),
        grad_kernel,
        grad_bias.reshape(GATES),
    )


def solution(mesh):
    lat, lon = mesh.shape["lat"], mesh.shape["lon"]
    sizes = {(16, 32): (4, 8, 2, 4), (4, 4): (2, 2, 1, 2)}[(lat, lon)]
    cells = P(None, "lat", "lon")
    flat = P("lat", "lon")
    return jax.shard_map(
        functools.partial(body, sizes),
        mesh=mesh,
        in_specs=(cells, cells, cells, P(), P(), P(), flat, flat, flat, cells),
        out_specs=(cells, cells, cells, cells, cells, P(), P()),
        check_vma=False,
    )
```

time: 80 us -> 63.6 us (0.80)
  local copies, waits for them, and re-layouts: 9.7 us -> 0 us
  Pallas kernels: 69.3 us -> 62.8 us
    unnamed x21 -> x0, local copies, waits for them, and re-layouts: 8.48 us -> none
    pallas_call x4 -> x2, Pallas kernels: 69.3 us -> 62.8 us  [the longest x1 61.4 us: body(): pl.pallas_call(functools.partial(step_kernel, sizes, scaling), out_shape=...]
where the time goes in v2:
time: 63.6 us; the launch traced here: 63.4 us
  Pallas kernels  62.8 us (99%)
  between operations  0.64 us (1%)
    pallas_call x1, Pallas kernels, body(): pl.pallas_call(functools.partial(step_kernel, sizes, scaling), out_shape=...  61.4 us
    pallas_call x1, Pallas kernels, body(): pl.pallas_call(finish_kernel, out_shape=[cells, wide_cells, cells, cells,...  1.39 us

profile of v2, /device:TPU:1, one launch (start us, length us, event | category | flops | bytes accessed | tf_op | source)
XLA Modules:
  0.0 63.4 jit_solution(12899763157431577073)
XLA Ops:
  0.6 61.4 %whole_step.1 = (bf16[64,8,128]{2,1,0:T(8,128)(2,1)S(1)}, f32[512,128]{1,0:T(8,128)S(1)}, bf16[64,8,128]{2,1,0:T(8,128)(2,1)S(1)}, bf16[64,8,128]{2,1,0:T(8,128)...) custom-call(bf16[64,8,128]{2,1,0:T(8,128)(2,1)} %below_hbm.1, ...), custom_call_target="tpu_custom_call" | custom-call | tf_op jit(solution)/shard_map/whole_step/pallas_call | solution.py:660
  62.0 1.4 %results.1 = (bf16[64,8,128]{2,1,0:T(8,128)(2,1)}, f32[512,128]{1,0:T(8,128)}, bf16[64,8,128]{2,1,0:T(8,128)(2,1)}, bf16[64,8,128]{2,1,0:T(8,128)(2,1)}, f32[512...) custom-call(bf16[64,8,128]{2,1,0:T(8,128)(2,1)S(1)} %get-tuple-element.21.hidden_next, ...), custom_call_target="tpu_custom_call" | custom-call | tf_op jit(solution)/shard_map/results/pallas_call | solution.py:717

commit v3 on v2

--- a/solution.py
+++ b/solution.py
@@ -18,6 +18,7 @@
 GATES = 256
 HALF = GATES // 2
 LANES = 128
+EDGE = 16
 VMEM_SPEC = pl.BlockSpec(memory_space=pltpu.VMEM)
 VMEM_LIMIT = 48 * 1024 * 1024
 
@@ -114,6 +115,15 @@
         remote(last, halo.at[1], send_sem.at[1], recv_sem.at[1], place.down()),
     ]
     return copies, waits
+
+
+def to_edge(total):
+    return jnp.transpose(total)[0:EDGE].astype(BF16)
+
+
+def from_edge(edge):
+    rest = jnp.zeros((LANES - EDGE, edge.shape[1]), F32)
+    return jnp.transpose(jnp.concatenate([edge.astype(F32), rest], axis=0))
 
 
 def collect(total, row, position, shift, lanes):
@@ -185,6 +195,8 @@
     kernel_acc,
     turned,
     low_rows,
+    field,
+    rims,
     low_halo,
     low_edges,
     low_sides,
@@ -213,9 +225,10 @@
     hid = hidden_next.shape[0]
     width = grad_inputs.shape[0]
     partner, _ = place.peer("core", 1)
-    devices = [partner] + place.around()
-    for axis in ("x", "y", "z"):
-        devices += [device for _, device, _ in place.peers(axis)]
+    devices = place.around()
+    for axis in ("z", "y", "x"):
+        devices += [device for _, device, _ in reversed(place.peers(axis))]
+    devices.append(partner)
     barrier = greet(devices)
     mine = pl.multiple_of(place.core * HALF, HALF)
     theirs = pl.multiple_of((1 - place.core) * HALF, HALF)
@@ -239,27 +252,31 @@
     def state_row(r):
         return wide[pl.ds(r, STATE, stride=ROWS), :]
 
+    for r in (0, ROWS - 1):
+        rows[r + 1] = state_row(r).astype(BF16)
+    pl.semaphore_wait(barrier, len(devices))
+    row_copies, row_waits = rows_out(place, rows.at[1], rows.at[ROWS], halo, row_send.at[0], row_recv.at[0])
+
     lanes = lane_ids((STATE, COLS))
     east = jnp.zeros((STATE, COLS), F32)
     west = jnp.zeros((STATE, COLS), F32)
     for r in range(ROWS):
         value = state_row(r)
-        rows[r + 1] = value.astype(BF16)
+        if 0 < r < ROWS - 1:
+            rows[r + 1] = value.astype(BF16)
         east = collect(east, value, r + 1, r + 2, lanes)
         west = collect(west, value, r + 1, r + 1, lanes)
-    edges[0] = east.astype(BF16)
-    edges[1] = west.astype(BF16)
+    edges[0] = to_edge(east)
+    edges[1] = to_edge(west)
+    col_copies = cols_out(place, edges, sides, col_send.at[0], col_recv.at[0])
+
     for load in loads[2:]:
         load.wait()
-    for t in range(9):
-        turned[t] = jnp.transpose(weights[t].astype(F32)).astype(BF16)
     wide_grad[...] = hidden_grad[...].astype(F32).reshape(hid * ROWS, COLS)
     bias_cols = jnp.transpose(jnp.broadcast_to(gate_bias[...], (LANES, GATES)))
     read_cols = jnp.transpose(jnp.broadcast_to(readout[...], (LANES, hid)))
-
-    pl.semaphore_wait(barrier, len(devices))
-    row_copies, row_waits = rows_out(place, rows.at[1], rows.at[ROWS], halo, row_send.at[0], row_recv.at[0])
-    col_copies = cols_out(place, edges, sides, col_send.at[0], col_recv.at[0])
+    for t in range(9):
+        turned[t] = jnp.transpose(weights[t].astype(F32)).astype(BF16)
 
     corner_east = jnp.zeros((STATE, COLS), F32)
     corner_west = jnp.zeros((STATE, COLS), F32)
@@ -268,22 +285,23 @@
         value = halo[slot].astype(F32)
         corner_east = collect(corner_east, value, position, position + 1, lanes)
         corner_west = collect(corner_west, value, position, position, lanes)
-    corner_edges[0] = corner_east.astype(BF16)
-    corner_edges[1] = corner_west.astype(BF16)
+    corner_edges[0] = to_edge(corner_east)
+    corner_edges[1] = to_edge(corner_west)
     corner_copies = cols_out(place, corner_edges, corners, col_send.at[1], col_recv.at[1])
     pending += row_copies + col_copies + corner_copies
 
-    def open_windows(position, low, side_refs):
+    def open_windows(position, low, low_side, high_side):
         value = low.astype(F32)
-        before, after = spread(value, side_refs[0].astype(F32), side_refs[1].astype(F32), lanes, position)
+        before, after = spread(value, low_side, high_side, lanes, position)
         windows[position, 0:STATE] = before.astype(BF16)
         windows[position, STATE : 2 * STATE] = low
         windows[position, 2 * STATE : 3 * STATE] = after.astype(BF16)
 
     for copy in col_copies:
         copy.wait_recv()
+    low_side, high_side = from_edge(sides[0]), from_edge(sides[1])
     for position in range(1, PADDED - 1):
-        open_windows(position, rows[position], sides)
+        open_windows(position, rows[position], low_side, high_side)
 
     flat = jnp.concatenate([weights[t] for t in range(9)], axis=1)
 
@@ -335,8 +353,9 @@
 
     for copy in corner_copies:
         copy.wait_recv()
-    open_windows(0, halo[0], corners)
-    open_windows(PADDED - 1, halo[1], corners)
+    low_side, high_side = from_edge(corners[0]), from_edge(corners[1])
+    open_windows(0, halo[0], low_side, high_side)
+    open_windows(PADDED - 1, halo[1], low_side, high_side)
     bias_total = cells_of(LATE, bias_total)
 
     pair_copies = []
@@ -404,40 +423,49 @@
         preferred_element_type=F32,
     )
     bias_copies = bias_start(0, "core", bias)
-    row_copies, row_waits = rows_out(
-        place, low_rows.at[0], low_rows.at[ROWS - 1], low_halo, row_send.at[1], row_recv.at[1]
-    )
     hidden_next[...] = wide[pl.ds(0, hid * ROWS), :].reshape(hid, ROWS, COLS).astype(BF16)
+
     gate_lanes = lane_ids((GATES, COLS))
     east = jnp.zeros((GATES, COLS), F32)
     west = jnp.zeros((GATES, COLS), F32)
     for r in range(ROWS):
         value = low_rows[r].astype(F32)
+        before = jnp.where(gate_lanes == 0, 0.0, pltpu.roll(value, 1, 1))
+        after = jnp.where(gate_lanes == COLS - 1, 0.0, pltpu.roll(value, COLS - 1, 1))
+        low_windows[r + 1, 0:GATES] = before.astype(BF16)
+        low_windows[r + 1, GATES : 2 * GATES] = low_rows[r]
+        low_windows[r + 1, 2 * GATES : 3 * GATES] = after.astype(BF16)
         east = collect(east, value, r + 1, r + 2, gate_lanes)
         west = collect(west, value, r + 1, r + 1, gate_lanes)
+    for slot, (value, last) in enumerate(((east, 2), (west, 0))):
+        shifts = jnp.concatenate([pltpu.roll(value, a % LANES, 1).astype(BF16) for a in (-1, 0, 1)], axis=0)
+        taps = jnp.concatenate([turned[3 * a + last] for a in range(3)], axis=1)
+        low_edges[slot] = to_edge(jnp.dot(taps, shifts, preferred_element_type=F32))
+    low_copies = cols_out(place, low_edges, low_sides, col_send.at[2], col_recv.at[2])
+
+    low_windows[0] = jnp.zeros((3 * GATES, COLS), BF16)
+    low_windows[PADDED - 1] = jnp.zeros((3 * GATES, COLS), BF16)
+    flipped = jnp.concatenate([turned[8 - q] for q in range(9)], axis=1)
+    for pair in range(ROWS // 2):
+        blocks = [low_windows[r : r + 3].reshape(9 * GATES, COLS) for r in (2 * pair, 2 * pair + 1)]
+        both = jnp.dot(flipped, jnp.concatenate(blocks, axis=1), preferred_element_type=F32)
+        for k in range(2):
+            field[2 * pair + k] = both[:, k * COLS : (k + 1) * COLS]
+    field[ROWS] = jnp.dot(flipped[:, 6 * GATES :], low_windows[1], preferred_element_type=F32)
+    field[ROWS + 1] = jnp.dot(flipped[:, : 3 * GATES], low_windows[ROWS], preferred_element_type=F32)
     bias = bias_finish(0, "core", bias_copies)
     bias_copies = bias_start(1, "x", bias)
-    for slot, position in ((0, 0), (1, PADDED - 1)):
-        row_waits[slot].wait_recv()
-        value = low_halo[slot].astype(F32)
-        east = collect(east, value, position, position + 1, gate_lanes)
-        west = collect(west, value, position, position, gate_lanes)
-    low_edges[0] = east.astype(BF16)
-    low_edges[1] = west.astype(BF16)
-    low_copies = cols_out(place, low_edges, low_sides, col_send.at[2], col_recv.at[2])
-    pending += row_copies + low_copies
-    bias = bias_finish(1, "x", bias_copies)
-    bias_copies = bias_start(2, "y", bias)
 
     second_copies = []
-    for a in (2, 0, 1):
+
+    def second_start(a):
         axis1, axis2, _ = ORDERS[a]
         n1, n2 = place.count[axis1], place.count[axis2]
         rows1 = HALF // n1
         rows2 = rows1 // n2
         for copy in reversed(first_copies[a]):
             copy.wait_recv()
-        pending += first_copies[a]
+        pending.extend(first_copies[a])
         start = pl.multiple_of(place.index[axis1] * rows1, rows1)
         total = owned[a, :, pl.ds(start, rows1), :]
         for k in range(n1 - 1):
@@ -451,8 +479,27 @@
             copies.append(copy)
         second_copies.append((a, copies))
 
-    bias = bias_finish(2, "y", bias_copies)
-    bias_copies = bias_start(3, "z", bias)
+    second_start(2)
+
+    for copy in low_copies:
+        copy.wait_recv()
+    low_side, high_side = from_edge(low_sides[0]), from_edge(low_sides[1])
+
+    def arrived(position):
+        first = jnp.where(lanes == 0, pltpu.roll(low_side, (-position) % LANES, 1), 0.0)
+        last = jnp.where(lanes == COLS - 1, pltpu.roll(high_side, (COLS - 1 - position) % LANES, 1), 0.0)
+        return first + last
+
+    rims[0] = (field[ROWS] + arrived(0)).astype(BF16)
+    rims[1] = (field[ROWS + 1] + arrived(PADDED - 1)).astype(BF16)
+    row_copies, row_waits = rows_out(place, rims.at[0], rims.at[1], low_halo, row_send.at[1], row_recv.at[1])
+    pending += low_copies + row_copies
+    second_start(0)
+    second_start(1)
+    for r in range(ROWS):
+        field[r] = field[r] + arrived(r + 1)
+    bias = bias_finish(1, "x", bias_copies)
+    bias_copies = bias_start(2, "y", bias)
 
     third_copies = []
     for a, copies2 in second_copies:
@@ -472,7 +519,8 @@
             copies.append(copy)
         third_copies.append((a, copies))
 
-    bias_sum[...] = bias_finish(3, "z", bias_copies) * scaling
+    bias = bias_finish(2, "y", bias_copies)
+    bias_copies = bias_start(3, "z", bias)
 
     fourth_copies = []
     for a, copies3 in third_copies:
@@ -484,7 +532,7 @@
         for k in range(1, place.count[axis3]):
             total = total + third[a][k]
         slot = place.index[axis2]
-        gathered[a][slot] = total * scaling
+        gathered[a][slot] = (total * scaling).astype(BF16)
         copies = []
         for k, device, _ in reversed(place.peers(axis2)):
             copy = remote(gathered[a].at[slot], gathered[a].at[slot], sends.at[4, a, k], recvs.at[4, a, k], device)
@@ -506,14 +554,16 @@
         last_copies.append(copy)
 
     fifth_copies = []
-    for a, copies4 in fourth_copies:
+    for a, copies4 in sorted(fourth_copies, key=lambda entry: entry[0]):
         axis1, axis2, _ = ORDERS[a]
         n1 = place.count[axis1]
         for copy in reversed(copies4):
             copy.wait_recv()
         pending += copies4
         block = block_of(a, place.index[axis1])
-        block[...] = jnp.concatenate([gathered[a][p] for p in range(place.count[axis2])], axis=1).astype(BF16)
+        block[...] = jnp.concatenate(
+            [gathered[a][p].astype(F32) for p in range(place.count[axis2])], axis=1
+        ).astype(BF16)
         copies = []
         for k, device, _ in reversed(place.peers(axis1)):
             copy = remote(block, block, sends.at[5, a, k], recvs.at[5, a, k], device)
@@ -522,50 +572,16 @@
         forward(a, place.index[axis1], n1 - 1)
         fifth_copies.append((a, copies))
 
-    for copy in low_copies:
-        copy.wait_recv()
-    low_side = low_sides[0].astype(F32)
-    high_side = low_sides[1].astype(F32)
-    for position in range(PADDED):
-        if position == 0:
-            low = low_halo[0]
-        elif position == PADDED - 1:
-            low = low_halo[1]
-        else:
-            low = low_rows[position - 1]
-        before, after = spread(low.astype(F32), low_side, high_side, gate_lanes, position)
-        low_windows[position, 0:GATES] = before.astype(BF16)
-        low_windows[position, GATES : 2 * GATES] = low
-        low_windows[position, 2 * GATES : 3 * GATES] = after.astype(BF16)
-    flipped = jnp.concatenate([turned[8 - q] for q in range(9)], axis=1)
-    for pair in range(ROWS // 2):
-        first = 2 * pair
-        blocks = []
-        for k in range(2):
-            r = first + k
-            pieces = [low_windows[r + d] for d in range(3)]
-            if r == 0:
-                pieces[0] = jnp.zeros_like(pieces[0])
-            if r == ROWS - 1:
-                pieces[2] = jnp.zeros_like(pieces[2])
-            blocks.append(jnp.concatenate(pieces, axis=0))
-        both = jnp.dot(flipped, jnp.concatenate(blocks, axis=1), preferred_element_type=F32)
-        for k in range(2):
-            r = first + k
-            value = both[:, k * COLS : (k + 1) * COLS]
-            if r == 0:
-                edge = [turned[jnp.where(place.north, 2 - q, 8 - q)] for q in range(3)]
-                value = value + jnp.dot(jnp.concatenate(edge, axis=1), low_windows[0], preferred_element_type=F32)
-            if r == ROWS - 1:
-                edge = [turned[jnp.where(place.south, 8 - q, 2 - q)] for q in range(3)]
-                value = value + jnp.dot(
-                    jnp.concatenate(edge, axis=1), low_windows[PADDED - 1], preferred_element_type=F32
-                )
-            wide[pl.ds(r, STATE, stride=ROWS), :] = value
+    bias_sum[...] = bias_finish(3, "z", bias_copies) * scaling
+    for slot, r in ((0, 0), (1, ROWS - 1)):
+        row_waits[slot].wait_recv()
+        field[r] = field[r] + low_halo[slot].astype(F32)
+    for r in range(ROWS):
+        wide[pl.ds(r, STATE, stride=ROWS), :] = field[r]
     grad_inputs[...] = wide[pl.ds(0, width * ROWS), :].reshape(width, ROWS, COLS).astype(BF16)
     grad_hidden[...] = wide[pl.ds(width * ROWS, hid * ROWS), :].reshape(hid, ROWS, COLS).astype(BF16)
 
-    for a, copies5 in fifth_copies:
+    for a, copies5 in fifth_copies[2:] + fifth_copies[:2]:
         for copy, k, sender in reversed(copies5):
             copy.wait_recv()
             forward(a, sender, k)
@@ -676,17 +692,19 @@
             pltpu.VMEM((hid * ROWS, COLS), F32),
             pltpu.VMEM((PADDED, STATE, COLS), BF16),
             pltpu.VMEM((2, STATE, COLS), BF16),
-            pltpu.VMEM((2, STATE, COLS), BF16),
-            pltpu.VMEM((2, STATE, COLS), BF16),
-            pltpu.VMEM((2, STATE, COLS), BF16),
-            pltpu.VMEM((2, STATE, COLS), BF16),
+            pltpu.VMEM((2, EDGE, STATE), BF16),
+            pltpu.VMEM((2, EDGE, STATE), BF16),
+            pltpu.VMEM((2, EDGE, STATE), BF16),
+            pltpu.VMEM((2, EDGE, STATE), BF16),
             pltpu.VMEM((PADDED, 3 * STATE, COLS), BF16),
             pltpu.VMEM((3, GATES, 3 * STATE), F32),
             pltpu.VMEM((9, STATE, GATES), BF16),
             pltpu.VMEM((ROWS, GATES, COLS), BF16),
-            pltpu.VMEM((2, GATES, COLS), BF16),
-            pltpu.VMEM((2, GATES, COLS), BF16),
-            pltpu.VMEM((2, GATES, COLS), BF16),
+            pltpu.VMEM((PADDED, STATE, COLS), F32),
+            pltpu.VMEM((2, STATE, COLS), BF16),
+            pltpu.VMEM((2, STATE, COLS), BF16),
+            pltpu.VMEM((2, EDGE, STATE), BF16),
+            pltpu.VMEM((2, EDGE, STATE), BF16),
             pltpu.VMEM((PADDED, 3 * GATES, COLS), BF16),
             pltpu.VMEM((3, 3, HALF, STATE), BF16),
             pltpu.VMEM((3, 3, HALF, STATE), BF16),
@@ -696,7 +714,7 @@
             [pltpu.VMEM((n2, 3, r2, STATE), F32) for _, _, n2, r2, _ in chunk],
             [pltpu.VMEM((n2 - 1, 3, r2, STATE), F32) for _, _, n2, r2, _ in chunk],
             [pltpu.VMEM((n3, 3, r2, STATE), F32) for _, _, _, r2, n3 in chunk],
-            [pltpu.VMEM((n2, 3, r2, STATE), F32) for _, _, n2, r2, _ in chunk],
+            [pltpu.VMEM((n2, 3, r2, STATE), BF16) for _, _, n2, r2, _ in chunk],
             [pltpu.VMEM((n, 8, GATES), F32) for n in (2, nx, ny, zh * zl)],
             dma((len(inputs),)),
             dma((2, 2)),

time: 63.6 us -> 56.2 us (0.88)
  Pallas kernels: 62.8 us -> 55.4 us
    pallas_call x1, Pallas kernels: 61.4 us -> 54 us  [body(): pl.pallas_call(functools.partial(step_kernel, sizes, scaling), out_shape=...]
where the time goes in v3:
time: 56.2 us; the launch traced here: 56 us
  Pallas kernels  55.4 us (99%)
  between operations  0.64 us (1%)
    pallas_call x1, Pallas kernels, body(): pl.pallas_call(functools.partial(step_kernel, sizes, scaling), out_shape=...  54 us
    pallas_call x1, Pallas kernels, body(): pl.pallas_call(finish_kernel, out_shape=[cells, wide_cells, cells, cells,...  1.39 us

profile of v3, /device:TPU:1, one launch (start us, length us, event | category | flops | bytes accessed | tf_op | source)
XLA Modules:
  0.0 56.0 jit_solution(14583222789596404987)
XLA Ops:
  0.6 54.0 %whole_step.1 = (bf16[64,8,128]{2,1,0:T(8,128)(2,1)S(1)}, f32[512,128]{1,0:T(8,128)S(1)}, bf16[64,8,128]{2,1,0:T(8,128)(2,1)S(1)}, bf16[64,8,128]{2,1,0:T(8,128)...) custom-call(bf16[64,8,128]{2,1,0:T(8,128)(2,1)} %below_hbm.1, ...), custom_call_target="tpu_custom_call" | custom-call | tf_op jit(solution)/shard_map/whole_step/pallas_call | solution.py:676
  54.6 1.4 %results.1 = (bf16[64,8,128]{2,1,0:T(8,128)(2,1)}, f32[512,128]{1,0:T(8,128)}, bf16[64,8,128]{2,1,0:T(8,128)(2,1)}, bf16[64,8,128]{2,1,0:T(8,128)(2,1)}, f32[512...) custom-call(bf16[64,8,128]{2,1,0:T(8,128)(2,1)S(1)} %get-tuple-element.21.hidden_next, ...), custom_call_target="tpu_custom_call" | custom-call | tf_op jit(solution)/shard_map/results/pallas_call | solution.py:735

commit v4 on v3

--- a/solution.py
+++ b/solution.py
@@ -480,6 +480,8 @@
         second_copies.append((a, copies))
 
     second_start(2)
+    second_start(0)
+    second_start(1)
 
     for copy in low_copies:
         copy.wait_recv()
@@ -494,8 +496,6 @@
     rims[1] = (field[ROWS + 1] + arrived(PADDED - 1)).astype(BF16)
     row_copies, row_waits = rows_out(place, rims.at[0], rims.at[1], low_halo, row_send.at[1], row_recv.at[1])
     pending += low_copies + row_copies
-    second_start(0)
-    second_start(1)
     for r in range(ROWS):
         field[r] = field[r] + arrived(r + 1)
     bias = bias_finish(1, "x", bias_copies)

time: 56.2 us -> 55.8 us (level)
  no operation moved by 1% of the time
where the time goes in v4:
time: 55.8 us; the launch traced here: 55.7 us
  Pallas kernels  55 us (99%)
  between operations  0.64 us (1%)
    pallas_call x1, Pallas kernels, body(): pl.pallas_call(functools.partial(step_kernel, sizes, scaling), out_shape=...  53.6 us
    pallas_call x1, Pallas kernels, body(): pl.pallas_call(finish_kernel, out_shape=[cells, wide_cells, cells, cells,...  1.39 us

profile of v4, /device:TPU:1, one launch (start us, length us, event | category | flops | bytes accessed | tf_op | source)
XLA Modules:
  0.0 55.7 jit_solution(1597556357410359452)
XLA Ops:
  0.6 53.6 %whole_step.1 = (bf16[64,8,128]{2,1,0:T(8,128)(2,1)S(1)}, f32[512,128]{1,0:T(8,128)S(1)}, bf16[64,8,128]{2,1,0:T(8,128)(2,1)S(1)}, bf16[64,8,128]{2,1,0:T(8,128)...) custom-call(bf16[64,8,128]{2,1,0:T(8,128)(2,1)} %below_hbm.1, ...), custom_call_target="tpu_custom_call" | custom-call | tf_op jit(solution)/shard_map/whole_step/pallas_call | solution.py:676
  54.3 1.4 %results.1 = (bf16[64,8,128]{2,1,0:T(8,128)(2,1)}, f32[512,128]{1,0:T(8,128)}, bf16[64,8,128]{2,1,0:T(8,128)(2,1)}, bf16[64,8,128]{2,1,0:T(8,128)(2,1)}, f32[512...) custom-call(bf16[64,8,128]{2,1,0:T(8,128)(2,1)S(1)} %get-tuple-element.21.hidden_next, ...), custom_call_target="tpu_custom_call" | custom-call | tf_op jit(solution)/shard_map/results/pallas_call | solution.py:735

commit v5 on v4

--- a/solution.py
+++ b/solution.py
@@ -76,7 +76,14 @@
         return (self.lat, lax.rem(self.lon + self.nlon - 1, self.nlon))
 
     def around(self):
-        return [self.up(), self.down(), self.east(), self.west()]
+        return [self.up(), self.down(), self.east(), self.west(), *self.diagonal()]
+
+    def diagonal(self):
+        found = []
+        for lat, lon in (self.up(), self.down()):
+            for steps in (1, self.nlon - 1):
+                found.append((lat, lax.rem(lon + steps, self.nlon)))
+        return found
 
 
 def greet(devices):
@@ -118,7 +125,19 @@
 
 
 def to_edge(total):
-    return jnp.transpose(total)[0:EDGE].astype(BF16)
+    return jnp.transpose(total)[0:EDGE]
+
+
+def corners_out(place, outgoing, corners, send_sem, recv_sem):
+    copies, waits = [], []
+    for i, device in enumerate(place.diagonal()):
+        slot = jnp.where(place.north, 0, 1) if i < 2 else jnp.where(place.south, 1, 0)
+        side = i % 2
+        copy = remote(outgoing.at[i], corners.at[slot, side], send_sem.at[i], recv_sem.at[slot, side], device)
+        copy.start()
+        copies.append(copy)
+        waits.append(remote(outgoing.at[i], corners.at[i // 2, side], send_sem.at[i], recv_sem.at[i // 2, side], device))
+    return copies, waits
 
 
 def from_edge(edge):
@@ -216,6 +235,8 @@
     row_recv,
     col_send,
     col_recv,
+    corner_send,
+    corner_recv,
     sends,
     recvs,
     bias_send,
@@ -266,9 +287,15 @@
             rows[r + 1] = value.astype(BF16)
         east = collect(east, value, r + 1, r + 2, lanes)
         west = collect(west, value, r + 1, r + 1, lanes)
-    edges[0] = to_edge(east)
-    edges[1] = to_edge(west)
+    ends = (to_edge(east), to_edge(west))
+    for i in range(4):
+        position = 1 if i < 2 else ROWS
+        corner_edges[i] = jnp.broadcast_to(ends[i % 2][position : position + 1], (8, STATE))
+    corner_copies, corner_waits = corners_out(place, corner_edges, corners, corner_send, corner_recv)
+    edges[0] = ends[0].astype(BF16)
+    edges[1] = ends[1].astype(BF16)
     col_copies = cols_out(place, edges, sides, col_send.at[0], col_recv.at[0])
+    pending += row_copies + col_copies + corner_copies
 
     for load in loads[2:]:
         load.wait()
@@ -278,21 +305,8 @@
     for t in range(9):
         turned[t] = jnp.transpose(weights[t].astype(F32)).astype(BF16)
 
-    corner_east = jnp.zeros((STATE, COLS), F32)
-    corner_west = jnp.zeros((STATE, COLS), F32)
-    for slot, position in ((0, 0), (1, PADDED - 1)):
-        row_waits[slot].wait_recv()
-        value = halo[slot].astype(F32)
-        corner_east = collect(corner_east, value, position, position + 1, lanes)
-        corner_west = collect(corner_west, value, position, position, lanes)
-    corner_edges[0] = to_edge(corner_east)
-    corner_edges[1] = to_edge(corner_west)
-    corner_copies = cols_out(place, corner_edges, corners, col_send.at[1], col_recv.at[1])
-    pending += row_copies + col_copies + corner_copies
-
     def open_windows(position, low, low_side, high_side):
-        value = low.astype(F32)
-        before, after = spread(value, low_side, high_side, lanes, position)
+        before, after = spread(low.astype(F32), low_side, high_side, lanes, position)
         windows[position, 0:STATE] = before.astype(BF16)
         windows[position, STATE : 2 * STATE] = low
         windows[position, 2 * STATE : 3 * STATE] = after.astype(BF16)
@@ -340,36 +354,40 @@
             low_rows[r] = pre_grad.astype(BF16)
         return bias_total
 
-    def kernel_terms(gates, rows_in, a):
-        cells = jnp.concatenate([low_rows[r, gates, :] for r in rows_in], axis=1)
+    def kernel_terms(cells, rows_in, a):
         seen = jnp.concatenate([windows[r + a] for r in rows_in], axis=1)
         return lax.dot_general(cells, seen, (((1,), (1,)), ((), ())), preferred_element_type=F32)
 
     bias_total = jnp.zeros((GATES, COLS), F32)
     for pair in EARLY:
         bias_total = cells_of(pair, bias_total)
+    cells = jnp.concatenate([low_rows[r] for r in range(1, ROWS - 1)], axis=1)
     for a in range(3):
-        kernel_acc[a] = kernel_terms(slice(None), range(1, ROWS - 1), a)
-
-    for copy in corner_copies:
-        copy.wait_recv()
-    low_side, high_side = from_edge(corners[0]), from_edge(corners[1])
-    open_windows(0, halo[0], low_side, high_side)
-    open_windows(PADDED - 1, halo[1], low_side, high_side)
+        kernel_acc[a] = kernel_terms(cells, range(1, ROWS - 1), a)
+
+    for wait in row_waits + corner_waits:
+        wait.wait_recv()
+    for slot, position in ((0, 0), (1, PADDED - 1)):
+        ends = [jnp.transpose(jnp.broadcast_to(corners[slot, side, 0:1], (LANES, STATE))) for side in range(2)]
+        open_windows(position, halo[slot], *ends)
     bias_total = cells_of(LATE, bias_total)
 
+    halves = [pl.ds(theirs, HALF), pl.ds(mine, HALF)]
+    cells = jnp.concatenate(
+        [jnp.concatenate([low_rows[r, half, :] for r in LATE], axis=1) for half in halves], axis=0
+    )
     pair_copies = []
     for a in range(3):
-        part = kernel_acc[a, pl.ds(theirs, HALF), :] + kernel_terms(pl.ds(theirs, HALF), LATE, a)
+        part = kernel_terms(cells, LATE, a)
+        given = part[0:HALF] + kernel_acc[a, halves[0], :]
+        kept = part[HALF:] + kernel_acc[a, halves[1], :]
         for b in range(3):
-            pair_out[a, b] = part[:, b * STATE : (b + 1) * STATE].astype(BF16)
+            pair_out[a, b] = given[:, b * STATE : (b + 1) * STATE].astype(BF16)
         copy = remote(pair_out.at[a], pair_in.at[a], sends.at[0, a, 0], recvs.at[0, a, 0], partner)
         copy.start()
         pair_copies.append(copy)
-    for a in range(3):
-        part = kernel_acc[a, pl.ds(mine, HALF), :] + kernel_terms(pl.ds(mine, HALF), LATE, a)
         for b in range(3):
-            owned[a, b] = part[:, b * STATE : (b + 1) * STATE]
+            owned[a, b] = kept[:, b * STATE : (b + 1) * STATE]
 
     first_copies = []
     for a in range(3):
@@ -440,7 +458,7 @@
     for slot, (value, last) in enumerate(((east, 2), (west, 0))):
         shifts = jnp.concatenate([pltpu.roll(value, a % LANES, 1).astype(BF16) for a in (-1, 0, 1)], axis=0)
         taps = jnp.concatenate([turned[3 * a + last] for a in range(3)], axis=1)
-        low_edges[slot] = to_edge(jnp.dot(taps, shifts, preferred_element_type=F32))
+        low_edges[slot] = to_edge(jnp.dot(taps, shifts, preferred_element_type=F32)).astype(BF16)
     low_copies = cols_out(place, low_edges, low_sides, col_send.at[2], col_recv.at[2])
 
     low_windows[0] = jnp.zeros((3 * GATES, COLS), BF16)
@@ -694,8 +712,8 @@
             pltpu.VMEM((2, STATE, COLS), BF16),
             pltpu.VMEM((2, EDGE, STATE), BF16),
             pltpu.VMEM((2, EDGE, STATE), BF16),
-            pltpu.VMEM((2, EDGE, STATE), BF16),
-            pltpu.VMEM((2, EDGE, STATE), BF16),
+            pltpu.VMEM((4, 8, STATE), F32),
+            pltpu.VMEM((2, 2, 8, STATE), F32),
             pltpu.VMEM((PADDED, 3 * STATE, COLS), BF16),
             pltpu.VMEM((3, GATES, 3 * STATE), F32),
             pltpu.VMEM((9, STATE, GATES), BF16),
@@ -721,6 +739,8 @@
             dma((2, 2)),
             dma((3, 2)),
             dma((3, 2)),
+            dma((4,)),
+            dma((2, 2)),
             dma((7, 3, most)),
             dma((7, 3, most)),
             dma((4, most)),

time: 55.8 us -> 54 us (0.968)
  Pallas kernels: 55 us -> 53.2 us
    pallas_call x1, Pallas kernels: 53.6 us -> 51.8 us  [body(): pl.pallas_call(functools.partial(step_kernel, sizes, scaling), out_shape=...]
where the time goes in v5:
time: 54 us; the launch traced here: 53.8 us
  Pallas kernels  53.2 us (99%)
  between operations  0.64 us (1%)
    pallas_call x1, Pallas kernels, body(): pl.pallas_call(functools.partial(step_kernel, sizes, scaling), out_shape=...  51.8 us
    pallas_call x1, Pallas kernels, body(): pl.pallas_call(finish_kernel, out_shape=[cells, wide_cells, cells, cells,...  1.39 us

profile of v5, /device:TPU:1, one launch (start us, length us, event | category | flops | bytes accessed | tf_op | source)
XLA Modules:
  0.0 53.8 jit_solution(6064960377375635594)
XLA Ops:
  0.6 51.8 %whole_step.1 = (bf16[64,8,128]{2,1,0:T(8,128)(2,1)S(1)}, f32[512,128]{1,0:T(8,128)S(1)}, bf16[64,8,128]{2,1,0:T(8,128)(2,1)S(1)}, bf16[64,8,128]{2,1,0:T(8,128)...) custom-call(bf16[64,8,128]{2,1,0:T(8,128)(2,1)} %below_hbm.1, ...), custom_call_target="tpu_custom_call" | custom-call | tf_op jit(solution)/shard_map/whole_step/pallas_call | solution.py:694
  52.4 1.4 %results.1 = (bf16[64,8,128]{2,1,0:T(8,128)(2,1)}, f32[512,128]{1,0:T(8,128)}, bf16[64,8,128]{2,1,0:T(8,128)(2,1)}, bf16[64,8,128]{2,1,0:T(8,128)(2,1)}, f32[512...) custom-call(bf16[64,8,128]{2,1,0:T(8,128)(2,1)S(1)} %get-tuple-element.21.hidden_next, ...), custom_call_target="tpu_custom_call" | custom-call | tf_op jit(solution)/shard_map/results/pallas_call | solution.py:755

commit v6 on v5

--- a/solution.py
+++ b/solution.py
@@ -215,6 +215,8 @@
     turned,
     low_rows,
     field,
+    low_corner_edges,
+    low_corners,
     rims,
     low_halo,
     low_edges,
@@ -237,6 +239,8 @@
     col_recv,
     corner_send,
     corner_recv,
+    low_corner_send,
+    low_corner_recv,
     sends,
     recvs,
     bias_send,
@@ -458,19 +462,26 @@
     for slot, (value, last) in enumerate(((east, 2), (west, 0))):
         shifts = jnp.concatenate([pltpu.roll(value, a % LANES, 1).astype(BF16) for a in (-1, 0, 1)], axis=0)
         taps = jnp.concatenate([turned[3 * a + last] for a in range(3)], axis=1)
-        low_edges[slot] = to_edge(jnp.dot(taps, shifts, preferred_element_type=F32)).astype(BF16)
+        given_cells = to_edge(jnp.dot(taps, shifts, preferred_element_type=F32))
+        low_edges[slot] = given_cells.astype(BF16)
+        for i, position in ((slot, 0), (slot + 2, PADDED - 1)):
+            low_corner_edges[i] = jnp.broadcast_to(given_cells[position : position + 1], (8, STATE))
     low_copies = cols_out(place, low_edges, low_sides, col_send.at[2], col_recv.at[2])
-
+    low_corner_copies, low_corner_waits = corners_out(
+        place, low_corner_edges, low_corners, low_corner_send, low_corner_recv
+    )
+
+    flipped = jnp.concatenate([turned[8 - q] for q in range(9)], axis=1)
+    rims[0] = jnp.dot(flipped[:, 6 * GATES :], low_windows[1], preferred_element_type=F32).astype(BF16)
+    rims[1] = jnp.dot(flipped[:, : 3 * GATES], low_windows[ROWS], preferred_element_type=F32).astype(BF16)
+    row_copies, row_waits = rows_out(place, rims.at[0], rims.at[1], low_halo, row_send.at[1], row_recv.at[1])
     low_windows[0] = jnp.zeros((3 * GATES, COLS), BF16)
     low_windows[PADDED - 1] = jnp.zeros((3 * GATES, COLS), BF16)
-    flipped = jnp.concatenate([turned[8 - q] for q in range(9)], axis=1)
     for pair in range(ROWS // 2):
         blocks = [low_windows[r : r + 3].reshape(9 * GATES, COLS) for r in (2 * pair, 2 * pair + 1)]
         both = jnp.dot(flipped, jnp.concatenate(blocks, axis=1), preferred_element_type=F32)
         for k in range(2):
             field[2 * pair + k] = both[:, k * COLS : (k + 1) * COLS]
-    field[ROWS] = jnp.dot(flipped[:, 6 * GATES :], low_windows[1], preferred_element_type=F32)
-    field[ROWS + 1] = jnp.dot(flipped[:, : 3 * GATES], low_windows[ROWS], preferred_element_type=F32)
     bias = bias_finish(0, "core", bias_copies)
     bias_copies = bias_start(1, "x", bias)
 
@@ -505,22 +516,19 @@
         copy.wait_recv()
     low_side, high_side = from_edge(low_sides[0]), from_edge(low_sides[1])
 
-    def arrived(position):
+    def arrived(low_side, high_side, position):
         first = jnp.where(lanes == 0, pltpu.roll(low_side, (-position) % LANES, 1), 0.0)
         last = jnp.where(lanes == COLS - 1, pltpu.roll(high_side, (COLS - 1 - position) % LANES, 1), 0.0)
         return first + last
 
-    rims[0] = (field[ROWS] + arrived(0)).astype(BF16)
-    rims[1] = (field[ROWS + 1] + arrived(PADDED - 1)).astype(BF16)
-    row_copies, row_waits = rows_out(place, rims.at[0], rims.at[1], low_halo, row_send.at[1], row_recv.at[1])
-    pending += low_copies + row_copies
+    pending += low_copies + row_copies + low_corner_copies
     for r in range(ROWS):
-        field[r] = field[r] + arrived(r + 1)
+        field[r] = field[r] + arrived(low_side, high_side, r + 1)
     bias = bias_finish(1, "x", bias_copies)
     bias_copies = bias_start(2, "y", bias)
 
     third_copies = []
-    for a, copies2 in second_copies:
+    for a, copies2 in sorted(second_copies, key=lambda entry: entry[0]):
         _, axis2, axis3 = ORDERS[a]
         for copy in reversed(copies2):
             copy.wait_recv()
@@ -572,7 +580,7 @@
         last_copies.append(copy)
 
     fifth_copies = []
-    for a, copies4 in sorted(fourth_copies, key=lambda entry: entry[0]):
+    for a, copies4 in fourth_copies:
         axis1, axis2, _ = ORDERS[a]
         n1 = place.count[axis1]
         for copy in reversed(copies4):
@@ -593,13 +601,17 @@
     bias_sum[...] = bias_finish(3, "z", bias_copies) * scaling
     for slot, r in ((0, 0), (1, ROWS - 1)):
         row_waits[slot].wait_recv()
-        field[r] = field[r] + low_halo[slot].astype(F32)
+        for wait in low_corner_waits[2 * slot : 2 * slot + 2]:
+            wait.wait_recv()
+        ends = [jnp.transpose(jnp.broadcast_to(low_corners[slot, side, 0:1], (LANES, STATE))) for side in range(2)]
+        given_cells = jnp.where(lanes == 0, ends[0], jnp.where(lanes == COLS - 1, ends[1], 0.0))
+        field[r] = field[r] + low_halo[slot].astype(F32) + given_cells
     for r in range(ROWS):
         wide[pl.ds(r, STATE, stride=ROWS), :] = field[r]
     grad_inputs[...] = wide[pl.ds(0, width * ROWS), :].reshape(width, ROWS, COLS).astype(BF16)
     grad_hidden[...] = wide[pl.ds(width * ROWS, hid * ROWS), :].reshape(hid, ROWS, COLS).astype(BF16)
 
-    for a, copies5 in fifth_copies[2:] + fifth_copies[:2]:
+    for a, copies5 in fifth_copies:
         for copy, k, sender in reversed(copies5):
             copy.wait_recv()
             forward(a, sender, k)
@@ -718,7 +730,9 @@
             pltpu.VMEM((3, GATES, 3 * STATE), F32),
             pltpu.VMEM((9, STATE, GATES), BF16),
             pltpu.VMEM((ROWS, GATES, COLS), BF16),
-            pltpu.VMEM((PADDED, STATE, COLS), F32),
+            pltpu.VMEM((ROWS, STATE, COLS), F32),
+            pltpu.VMEM((4, 8, STATE), F32),
+            pltpu.VMEM((2, 2, 8, STATE), F32),
             pltpu.VMEM((2, STATE, COLS), BF16),
             pltpu.VMEM((2, STATE, COLS), BF16),
             pltpu.VMEM((2, EDGE, STATE), BF16),
@@ -739,6 +753,8 @@
             dma((2, 2)),
             dma((3, 2)),
             dma((3, 2)),
+            dma((4,)),
+            dma((2, 2)),
             dma((4,)),
             dma((2, 2)),
             dma((7, 3, most)),

time: 54 us -> 53.7 us (level)
  no operation moved by 1% of the time
where the time goes in v6:
time: 53.7 us; the launch traced here: 53.6 us
  Pallas kernels  52.9 us (99%)
  between operations  0.64 us (1%)
    pallas_call x1, Pallas kernels, body(): pl.pallas_call(functools.partial(step_kernel, sizes, scaling), out_shape=...  51.6 us
    pallas_call x1, Pallas kernels, body(): pl.pallas_call(finish_kernel, out_shape=[cells, wide_cells, cells, cells,...  1.39 us

profile of v6, /device:TPU:1, one launch (start us, length us, event | category | flops | bytes accessed | tf_op | source)
XLA Modules:
  0.0 53.6 jit_solution(9506667616921443637)
XLA Ops:
  0.6 51.6 %whole_step.1 = (bf16[64,8,128]{2,1,0:T(8,128)(2,1)S(1)}, f32[512,128]{1,0:T(8,128)S(1)}, bf16[64,8,128]{2,1,0:T(8,128)(2,1)S(1)}, bf16[64,8,128]{2,1,0:T(8,128)...) custom-call(bf16[64,8,128]{2,1,0:T(8,128)(2,1)} %below_hbm.1, ...), custom_call_target="tpu_custom_call" | custom-call | tf_op jit(solution)/shard_map/whole_step/pallas_call | solution.py:706
  52.2 1.4 %results.1 = (bf16[64,8,128]{2,1,0:T(8,128)(2,1)}, f32[512,128]{1,0:T(8,128)}, bf16[64,8,128]{2,1,0:T(8,128)(2,1)}, bf16[64,8,128]{2,1,0:T(8,128)(2,1)}, f32[512...) custom-call(bf16[64,8,128]{2,1,0:T(8,128)(2,1)S(1)} %get-tuple-element.21.hidden_next, ...), custom_call_target="tpu_custom_call" | custom-call | tf_op jit(solution)/shard_map/results/pallas_call | solution.py:771

commit v7 on v6

--- a/solution.py
+++ b/solution.py
@@ -445,7 +445,6 @@
         preferred_element_type=F32,
     )
     bias_copies = bias_start(0, "core", bias)
-    hidden_next[...] = wide[pl.ds(0, hid * ROWS), :].reshape(hid, ROWS, COLS).astype(BF16)
 
     gate_lanes = lane_ids((GATES, COLS))
     east = jnp.zeros((GATES, COLS), F32)
@@ -475,13 +474,6 @@
     rims[0] = jnp.dot(flipped[:, 6 * GATES :], low_windows[1], preferred_element_type=F32).astype(BF16)
     rims[1] = jnp.dot(flipped[:, : 3 * GATES], low_windows[ROWS], preferred_element_type=F32).astype(BF16)
     row_copies, row_waits = rows_out(place, rims.at[0], rims.at[1], low_halo, row_send.at[1], row_recv.at[1])
-    low_windows[0] = jnp.zeros((3 * GATES, COLS), BF16)
-    low_windows[PADDED - 1] = jnp.zeros((3 * GATES, COLS), BF16)
-    for pair in range(ROWS // 2):
-        blocks = [low_windows[r : r + 3].reshape(9 * GATES, COLS) for r in (2 * pair, 2 * pair + 1)]
-        both = jnp.dot(flipped, jnp.concatenate(blocks, axis=1), preferred_element_type=F32)
-        for k in range(2):
-            field[2 * pair + k] = both[:, k * COLS : (k + 1) * COLS]
     bias = bias_finish(0, "core", bias_copies)
     bias_copies = bias_start(1, "x", bias)
 
@@ -512,18 +504,6 @@
     second_start(0)
     second_start(1)
 
-    for copy in low_copies:
-        copy.wait_recv()
-    low_side, high_side = from_edge(low_sides[0]), from_edge(low_sides[1])
-
-    def arrived(low_side, high_side, position):
-        first = jnp.where(lanes == 0, pltpu.roll(low_side, (-position) % LANES, 1), 0.0)
-        last = jnp.where(lanes == COLS - 1, pltpu.roll(high_side, (COLS - 1 - position) % LANES, 1), 0.0)
-        return first + last
-
-    pending += low_copies + row_copies + low_corner_copies
-    for r in range(ROWS):
-        field[r] = field[r] + arrived(low_side, high_side, r + 1)
     bias = bias_finish(1, "x", bias_copies)
     bias_copies = bias_start(2, "y", bias)
 
@@ -545,6 +525,26 @@
             copies.append(copy)
         third_copies.append((a, copies))
 
+    hidden_next[...] = wide[pl.ds(0, hid * ROWS), :].reshape(hid, ROWS, COLS).astype(BF16)
+    low_windows[0] = jnp.zeros((3 * GATES, COLS), BF16)
+    low_windows[PADDED - 1] = jnp.zeros((3 * GATES, COLS), BF16)
+    for pair in range(ROWS // 2):
+        blocks = [low_windows[r : r + 3].reshape(9 * GATES, COLS) for r in (2 * pair, 2 * pair + 1)]
+        both = jnp.dot(flipped, jnp.concatenate(blocks, axis=1), preferred_element_type=F32)
+        for k in range(2):
+            field[2 * pair + k] = both[:, k * COLS : (k + 1) * COLS]
+    for copy in low_copies:
+        copy.wait_recv()
+    low_side, high_side = from_edge(low_sides[0]), from_edge(low_sides[1])
+
+    def arrived(low_side, high_side, position):
+        first = jnp.where(lanes == 0, pltpu.roll(low_side, (-position) % LANES, 1), 0.0)
+        last = jnp.where(lanes == COLS - 1, pltpu.roll(high_side, (COLS - 1 - position) % LANES, 1), 0.0)
+        return first + last
+
+    pending += low_copies + row_copies + low_corner_copies
+    for r in range(ROWS):
+        field[r] = field[r] + arrived(low_side, high_side, r + 1)
     bias = bias_finish(2, "y", bias_copies)
     bias_copies = bias_start(3, "z", bias)
 
@@ -598,7 +598,6 @@
         forward(a, place.index[axis1], n1 - 1)
         fifth_copies.append((a, copies))
 
-    bias_sum[...] = bias_finish(3, "z", bias_copies) * scaling
     for slot, r in ((0, 0), (1, ROWS - 1)):
         row_waits[slot].wait_recv()
         for wait in low_corner_waits[2 * slot : 2 * slot + 2]:
@@ -616,6 +615,7 @@
             copy.wait_recv()
             forward(a, sender, k)
             pending.append(copy)
+    bias_sum[...] = bias_finish(3, "z", bias_copies) * scaling
     for copy in last_copies:
         copy.wait_recv()
     pending += last_copies

time: 53.7 us -> 53.8 us (level)
  no operation moved by 1% of the time
where the time goes in v7:
time: 53.8 us; the launch traced here: 53.6 us
  Pallas kernels  53 us (99%)
  between operations  0.64 us (1%)
    pallas_call x1, Pallas kernels, body(): pl.pallas_call(functools.partial(step_kernel, sizes, scaling), out_shape=...  51.6 us
    pallas_call x1, Pallas kernels, body(): pl.pallas_call(finish_kernel, out_shape=[cells, wide_cells, cells, cells,...  1.39 us

profile of v7, /device:TPU:1, one launch (start us, length us, event | category | flops | bytes accessed | tf_op | source)
XLA Modules:
  0.0 53.6 jit_solution(2247921406057943447)
XLA Ops:
  0.6 51.6 %whole_step.1 = (bf16[64,8,128]{2,1,0:T(8,128)(2,1)S(1)}, f32[512,128]{1,0:T(8,128)S(1)}, bf16[64,8,128]{2,1,0:T(8,128)(2,1)S(1)}, bf16[64,8,128]{2,1,0:T(8,128)...) custom-call(bf16[64,8,128]{2,1,0:T(8,128)(2,1)} %below_hbm.1, ...), custom_call_target="tpu_custom_call" | custom-call | tf_op jit(solution)/shard_map/whole_step/pallas_call | solution.py:706
  52.2 1.4 %results.1 = (bf16[64,8,128]{2,1,0:T(8,128)(2,1)}, f32[512,128]{1,0:T(8,128)}, bf16[64,8,128]{2,1,0:T(8,128)(2,1)}, bf16[64,8,128]{2,1,0:T(8,128)(2,1)}, f32[512...) custom-call(bf16[64,8,128]{2,1,0:T(8,128)(2,1)S(1)} %get-tuple-element.21.hidden_next, ...), custom_call_target="tpu_custom_call" | custom-call | tf_op jit(solution)/shard_map/results/pallas_call | solution.py:771

commit v8 on v7

--- a/solution.py
+++ b/solution.py
@@ -517,7 +517,7 @@
         for k in range(place.count[axis2] - 1):
             total = total + second_in[a][k]
         slot = place.index[axis3]
-        third[a][slot] = total
+        third[a][slot] = total.astype(BF16)
         copies = []
         for k, device, _ in reversed(place.peers(axis3)):
             copy = remote(third[a].at[slot], third[a].at[slot], sends.at[3, a, k], recvs.at[3, a, k], device)
@@ -554,9 +554,9 @@
         for copy in reversed(copies3):
             copy.wait_recv()
         pending += copies3
-        total = third[a][0]
+        total = third[a][0].astype(F32)
         for k in range(1, place.count[axis3]):
-            total = total + third[a][k]
+            total = total + third[a][k].astype(F32)
         slot = place.index[axis2]
         gathered[a][slot] = (total * scaling).astype(BF16)
         copies = []
@@ -745,7 +745,7 @@
             [pltpu.VMEM((n1 - 1, 3, r1, STATE), BF16) for n1, r1, _, _, _ in chunk],
             [pltpu.VMEM((n2, 3, r2, STATE), F32) for _, _, n2, r2, _ in chunk],
             [pltpu.VMEM((n2 - 1, 3, r2, STATE), F32) for _, _, n2, r2, _ in chunk],
-            [pltpu.VMEM((n3, 3, r2, STATE), F32) for _, _, _, r2, n3 in chunk],
+            [pltpu.VMEM((n3, 3, r2, STATE), BF16) for _, _, _, r2, n3 in chunk],
             [pltpu.VMEM((n2, 3, r2, STATE), BF16) for _, _, n2, r2, _ in chunk],
             [pltpu.VMEM((n, 8, GATES), F32) for n in (2, nx, ny, zh * zl)],
             dma((len(inputs),)),

time: 53.8 us -> 53.4 us (level)
  no operation moved by 1% of the time
where the time goes in v8:
time: 53.4 us; the launch traced here: 53.3 us
  Pallas kernels  52.6 us (99%)
  between operations  0.64 us (1%)
    pallas_call x1, Pallas kernels, body(): pl.pallas_call(functools.partial(step_kernel, sizes, scaling), out_shape=...  51.3 us
    pallas_call x1, Pallas kernels, body(): pl.pallas_call(finish_kernel, out_shape=[cells, wide_cells, cells, cells,...  1.39 us

profile of v8, /device:TPU:1, one launch (start us, length us, event | category | flops | bytes accessed | tf_op | source)
XLA Modules:
  0.0 53.3 jit_solution(18432803131271603488)
XLA Ops:
  0.6 51.3 %whole_step.1 = (bf16[64,8,128]{2,1,0:T(8,128)(2,1)S(1)}, f32[512,128]{1,0:T(8,128)S(1)}, bf16[64,8,128]{2,1,0:T(8,128)(2,1)S(1)}, bf16[64,8,128]{2,1,0:T(8,128)...) custom-call(bf16[64,8,128]{2,1,0:T(8,128)(2,1)} %below_hbm.1, ...), custom_call_target="tpu_custom_call" | custom-call | tf_op jit(solution)/shard_map/whole_step/pallas_call | solution.py:706
  51.9 1.4 %results.1 = (bf16[64,8,128]{2,1,0:T(8,128)(2,1)}, f32[512,128]{1,0:T(8,128)}, bf16[64,8,128]{2,1,0:T(8,128)(2,1)}, bf16[64,8,128]{2,1,0:T(8,128)(2,1)}, f32[512...) custom-call(bf16[64,8,128]{2,1,0:T(8,128)(2,1)S(1)} %get-tuple-element.21.hidden_next, ...), custom_call_target="tpu_custom_call" | custom-call | tf_op jit(solution)/shard_map/results/pallas_call | solution.py:771

commit v9 on v7

--- a/solution.py
+++ b/solution.py
@@ -610,11 +610,14 @@
     grad_inputs[...] = wide[pl.ds(0, width * ROWS), :].reshape(width, ROWS, COLS).astype(BF16)
     grad_hidden[...] = wide[pl.ds(width * ROWS, hid * ROWS), :].reshape(hid, ROWS, COLS).astype(BF16)
 
+    arrivals = []
     for a, copies5 in fifth_copies:
-        for copy, k, sender in reversed(copies5):
-            copy.wait_recv()
-            forward(a, sender, k)
-            pending.append(copy)
+        count = place.count[ORDERS[a][0]]
+        arrivals += [(min(k + 1, count - 1 - k), a, copy, k, sender) for copy, k, sender in copies5]
+    for _, a, copy, k, sender in sorted(arrivals, key=lambda entry: entry[:2]):
+        copy.wait_recv()
+        forward(a, sender, k)
+        pending.append(copy)
     bias_sum[...] = bias_finish(3, "z", bias_copies) * scaling
     for copy in last_copies:
         copy.wait_recv()

time: 53.8 us -> 53.9 us (level)
  no operation moved by 1% of the time
where the time goes in v9:
time: 53.9 us; the launch traced here: 53.7 us
  Pallas kernels  53.1 us (99%)
  between operations  0.64 us (1%)
    pallas_call x1, Pallas kernels, body(): pl.pallas_call(functools.partial(step_kernel, sizes, scaling), out_shape=...  51.7 us
    pallas_call x1, Pallas kernels, body(): pl.pallas_call(finish_kernel, out_shape=[cells, wide_cells, cells, cells,...  1.39 us

profile of v9, /device:TPU:1, one launch (start us, length us, event | category | flops | bytes accessed | tf_op | source)
XLA Modules:
  0.0 53.7 jit_solution(3513700756650689713)
XLA Ops:
  0.6 51.7 %whole_step.1 = (bf16[64,8,128]{2,1,0:T(8,128)(2,1)S(1)}, f32[512,128]{1,0:T(8,128)S(1)}, bf16[64,8,128]{2,1,0:T(8,128)(2,1)S(1)}, bf16[64,8,128]{2,1,0:T(8,128)...) custom-call(bf16[64,8,128]{2,1,0:T(8,128)(2,1)} %below_hbm.1, ...), custom_call_target="tpu_custom_call" | custom-call | tf_op jit(solution)/shard_map/whole_step/pallas_call | solution.py:709
  52.3 1.4 %results.1 = (bf16[64,8,128]{2,1,0:T(8,128)(2,1)}, f32[512,128]{1,0:T(8,128)}, bf16[64,8,128]{2,1,0:T(8,128)(2,1)}, bf16[64,8,128]{2,1,0:T(8,128)(2,1)}, f32[512...) custom-call(bf16[64,8,128]{2,1,0:T(8,128)(2,1)S(1)} %get-tuple-element.21.hidden_next, ...), custom_call_target="tpu_custom_call" | custom-call | tf_op jit(solution)/shard_map/results/pallas_call | solution.py:774

commit v10 on v9

--- a/solution.py
+++ b/solution.py
@@ -380,8 +380,8 @@
     cells = jnp.concatenate(
         [jnp.concatenate([low_rows[r, half, :] for r in LATE], axis=1) for half in halves], axis=0
     )
-    pair_copies = []
-    for a in range(3):
+    pair_copies = {}
+    for a in (2, 0, 1):
         part = kernel_terms(cells, LATE, a)
         given = part[0:HALF] + kernel_acc[a, halves[0], :]
         kept = part[HALF:] + kernel_acc[a, halves[1], :]
@@ -389,12 +389,12 @@
             pair_out[a, b] = given[:, b * STATE : (b + 1) * STATE].astype(BF16)
         copy = remote(pair_out.at[a], pair_in.at[a], sends.at[0, a, 0], recvs.at[0, a, 0], partner)
         copy.start()
-        pair_copies.append(copy)
+        pair_copies[a] = copy
         for b in range(3):
             owned[a, b] = kept[:, b * STATE : (b + 1) * STATE]
 
-    first_copies = []
-    for a in range(3):
+    first_copies = {}
+    for a in (2, 0, 1):
         pair_copies[a].wait_recv()
         total = owned[a] + pair_in[a].astype(F32)
         owned[a] = total
@@ -413,8 +413,8 @@
             )
             copy.start()
             copies.append(copy)
-        first_copies.append(copies)
-    pending += pair_copies
+        first_copies[a] = copies
+    pending += pair_copies.values()
 
     def bias_start(stage, axis, value):
         slot = place.index[axis]

time: 53.9 us -> 53.5 us (level)
  no operation moved by 1% of the time
where the time goes in v10:
time: 53.5 us; the launch traced here: 53.4 us
  Pallas kernels  52.8 us (99%)
  between operations  0.64 us (1%)
    pallas_call x1, Pallas kernels, body(): pl.pallas_call(functools.partial(step_kernel, sizes, scaling), out_shape=...  51.4 us
    pallas_call x1, Pallas kernels, body(): pl.pallas_call(finish_kernel, out_shape=[cells, wide_cells, cells, cells,...  1.39 us

profile of v10, /device:TPU:1, one launch (start us, length us, event | category | flops | bytes accessed | tf_op | source)
XLA Modules:
  0.0 53.4 jit_solution(6083101397064555046)
XLA Ops:
  0.6 51.4 %whole_step.1 = (bf16[64,8,128]{2,1,0:T(8,128)(2,1)S(1)}, f32[512,128]{1,0:T(8,128)S(1)}, bf16[64,8,128]{2,1,0:T(8,128)(2,1)S(1)}, bf16[64,8,128]{2,1,0:T(8,128)...) custom-call(bf16[64,8,128]{2,1,0:T(8,128)(2,1)} %below_hbm.1, ...), custom_call_target="tpu_custom_call" | custom-call | tf_op jit(solution)/shard_map/whole_step/pallas_call | solution.py:709
  52.0 1.4 %results.1 = (bf16[64,8,128]{2,1,0:T(8,128)(2,1)}, f32[512,128]{1,0:T(8,128)}, bf16[64,8,128]{2,1,0:T(8,128)(2,1)}, bf16[64,8,128]{2,1,0:T(8,128)(2,1)}, f32[512...) custom-call(bf16[64,8,128]{2,1,0:T(8,128)(2,1)S(1)} %get-tuple-element.21.hidden_next, ...), custom_call_target="tpu_custom_call" | custom-call | tf_op jit(solution)/shard_map/results/pallas_call | solution.py:774
